TPU v7x, 32 devices: a whole 2x2x4 slice. The times are simulated.
32 devices in a mesh: fsdp: 4 (over y, x), ctx: 8 (over z, core).
Axes of the slice: x: 2, y: 2, z: 4, core: 2. Of those that a mesh axis runs over, the one named last changes fastest.
Arguments:
- inputs: bfloat16 [4, 2048, 768], P('fsdp', 'ctx'), may hold values from -6 to 6
- lengths: int32 [4], P('fsdp'), may hold values from 128 to 2048
- cotangent: bfloat16 [4, 2048, 768], P('fsdp', 'ctx'), may hold values from -6 to 6
- query_key_value: bfloat16 [768, 2304], P('fsdp'), may hold values from -0.21875 to 0.21875
- query_bias: bfloat16 [768], P('fsdp'), may hold values from -3 to 3
- value_bias: bfloat16 [768], P('fsdp'), may hold values from -0.125 to 0.125
- output_weight: bfloat16 [768, 768], P('fsdp'), may hold values from -3.5 to 3.5
- output_bias: bfloat16 [768], P('fsdp'), may hold values from -3 to 3
- first_gain: bfloat16 [768], P('fsdp'), may hold values from 0.5 to 1.5
- first_shift: bfloat16 [768], P('fsdp'), may hold values from -3 to 3
- hidden_weight: bfloat16 [768, 3072], P('fsdp'), may hold values from -0.21875 to 0.21875
- hidden_bias: bfloat16 [3072], P('fsdp'), may hold values from -3 to 3
- down_weight: bfloat16 [3072, 768], P('fsdp'), may hold values from -0.109375 to 0.109375
- down_bias: bfloat16 [768], P('fsdp'), may hold values from -3 to 3
- second_gain: bfloat16 [768], P('fsdp'), may hold values from 0.5 to 1.5
- second_shift: bfloat16 [768], P('fsdp'), may hold values from -3 to 3
Outputs:
- outputs: bfloat16 [4, 2048, 768], P('fsdp', 'ctx')
- input_grad: float32 [4, 2048, 768], P('fsdp', 'ctx')
- query_key_value_grad: float32 [768, 2304], P('fsdp')
- query_bias_grad: float32 [768], P('fsdp')
- value_bias_grad: float32 [768], P('fsdp')
- output_weight_grad: float32 [768, 768], P('fsdp')
- output_bias_grad: float32 [768], P('fsdp')
- first_gain_grad: float32 [768], P('fsdp')
- first_shift_grad: float32 [768], P('fsdp')
- hidden_weight_grad: float32 [768, 3072], P('fsdp')
- hidden_bias_grad: float32 [3072], P('fsdp')
- down_weight_grad: float32 [3072, 768], P('fsdp')
- down_bias_grad: float32 [768], P('fsdp')
- second_gain_grad: float32 [768], P('fsdp')
- second_shift_grad: float32 [768], P('fsdp')
All inputs are finite; a program needn't handle non-finite values.
Results may differ from a plain program's by a relative error of at most 0.035.
Values may be sent and summed in bfloat16 or wider, within the bound.
No kernel may reach another device: no remote copies, remote signals or barrier semaphores. Data moves between devices by JAX's collectives and lax.ppermute only.
A program may use at most 128 MiB of HBM per device.

v0:
```python
import functools
import math

import jax
import jax.numpy as jnp
from jax import lax
from jax.experimental import pallas as pl
from jax.experimental.pallas import tpu as pltpu
from jax.sharding import PartitionSpec as P


H = 12
HD = 64
LANES = 128

EPSILON = 1e-12
MASKED = -1e30


def contract_rows(left, right):
    return lax.dot_general(
        left, right, (((0,), (0,)), ((), ())), preferred_element_type=jnp.float32
    )


def contract_cols(left, right):
    return lax.dot_general(
        left, right, (((1,), (1,)), ((), ())), preferred_element_type=jnp.float32
    )


def layer_norm(summed, norm_gain, norm_shift):
    row_mean = jnp.mean(summed, axis=-1, keepdims=True)
    centred = summed - row_mean
    variance = jnp.mean(centred * centred, axis=-1, keepdims=True)
    inv_std = lax.rsqrt(variance + EPSILON)
    scaled = centred * inv_std
    return (scaled * norm_gain + norm_shift, scaled, inv_std)


def norm_grad(out_grad, scaled, inv_std, norm_gain):
    gained = out_grad * norm_gain
    return inv_std * (
        gained
        - jnp.mean(gained, axis=-1, keepdims=True)
        - scaled * jnp.mean(gained * scaled, axis=-1, keepdims=True)
    )


def gelu_exact(values):
    return jax.nn.gelu(values, approximate=False)


def three_parts(column):
    high = column.astype(jnp.bfloat16).astype(jnp.float32)
    rest = column - high
    middle = rest.astype(jnp.bfloat16).astype(jnp.float32)
    return high, middle, rest - middle


def forward_kernel(q_ref, own_ref, far_ref, low_ref, o_ref, q2_ref, *, heads):
    for h in range(heads):
        here = slice(h * LANES, (h + 1) * LANES)
        there = slice((heads + h) * LANES, (heads + h + 1) * LANES)
        q = q_ref[0, :, here]
        s_own = contract_cols(q, own_ref[0, :, here])
        s_far = contract_cols(q, far_ref[0, :, here])
        row_max = jnp.maximum(
            jnp.max(s_own, axis=-1, keepdims=True), jnp.max(s_far, axis=-1, keepdims=True)
        )
        e_own = jnp.exp(s_own - row_max).astype(jnp.bfloat16)
        e_far = jnp.exp(s_far - row_max).astype(jnp.bfloat16)
        acc = jnp.dot(e_own, own_ref[0, :, there], preferred_element_type=jnp.float32)
        acc += jnp.dot(e_far, far_ref[0, :, there], preferred_element_type=jnp.float32)
        total = acc[:, HD : HD + 1]
        lane = lax.broadcasted_iota(jnp.int32, acc.shape, 1)
        out = jnp.where(lane < HD, acc / total, acc)
        o_ref[0, :, here] = out
        low_ref[0, :, h * HD : (h + 1) * HD] = out[:, :HD].astype(jnp.bfloat16)
        high, middle, low = three_parts(-row_max)
        wide = jnp.where(
            lane == HD + 1,
            high,
            jnp.where(
                lane == HD + 2, middle, jnp.where(lane == HD + 3, low, q.astype(jnp.float32))
            ),
        )
        q2_ref[0, :, here] = wide.astype(jnp.bfloat16)


def attend(q, own, far, block):
    seqs, rows, wide = q.shape
    heads = wide // LANES
    keys = rows + far.shape[1]
    blockwise = pl.BlockSpec((1, block, wide), lambda s, i: (s, i, 0))
    return pl.pallas_call(
        functools.partial(forward_kernel, heads=heads),
        grid=(seqs, rows // block),
        in_specs=[
            blockwise,
            pl.BlockSpec((1, rows, 2 * wide), lambda s, i: (s, 0, 0)),
            pl.BlockSpec((1, far.shape[1], 2 * wide), lambda s, i: (s, 0, 0)),
        ],
        out_specs=[
            pl.BlockSpec((1, block, heads * HD), lambda s, i: (s, i, 0)),
            blockwise,
            blockwise,
        ],
        out_shape=[
            jax.ShapeDtypeStruct((seqs, rows, heads * HD), jnp.bfloat16),
            jax.ShapeDtypeStruct((seqs, rows, wide), jnp.float32),
            jax.ShapeDtypeStruct((seqs, rows, wide), jnp.bfloat16),
        ],
        cost_estimate=pl.CostEstimate(
            flops=seqs * heads * rows * keys * 512,
            transcendentals=seqs * heads * rows * keys,
            bytes_accessed=seqs * heads * (rows + keys) * 1024,
        ),
    )(q, own, far)


def backward_kernel(
    q_ref,
    o_ref,
    g_ref,
    k_own,
    v_own,
    k_far,
    v_far,
    dq_ref,
    dk_own,
    dv_own,
    dk_far,
    dv_far,
    dk_own_acc,
    dv_own_acc,
    dk_far_acc,
    dv_far_acc,
    *,
    head,
    chunk,
):
    step = pl.program_id(1)
    q = q_ref[0]
    o = o_ref[0]
    g = g_ref[0, :, head * HD : (head + 1) * HD].astype(jnp.float32)
    g = jnp.concatenate([g, jnp.zeros_like(g)], axis=-1)
    total = o[:, HD : HD + 1]
    lane = lax.broadcasted_iota(jnp.int32, o.shape, 1)
    coef = jnp.sum(g * o, axis=-1, keepdims=True) / total
    high, middle, low = three_parts(-coef)
    un = jnp.where(
        lane == HD,
        high,
        jnp.where(lane == HD + 1, middle, jnp.where(lane == HD + 2, low, g / total)),
    ).astype(jnp.bfloat16)
    dq_t = jnp.zeros((LANES, q.shape[0]), jnp.float32)
    last = step == pl.num_programs(1) - 1
    for k_ref, v_ref, dk_ref, dv_ref, dk_acc, dv_acc in (
        (k_own, v_own, dk_own, dv_own, dk_own_acc, dv_own_acc),
        (k_far, v_far, dk_far, dv_far, dk_far_acc, dv_far_acc),
    ):

        @pl.when(step == 0)
        def _():
            dk_acc[...] = jnp.zeros_like(dk_acc)
            dv_acc[...] = jnp.zeros_like(dv_acc)

        def keys_step(index, dq_sum):
            rows = pl.ds(pl.multiple_of(index * chunk, chunk), chunk)
            k = k_ref[0, rows, :]
            e = jnp.exp(contract_cols(k, q))
            gp = contract_cols(v_ref[0, rows, :], un)
            ds = (e * gp).astype(jnp.bfloat16)
            dv_acc[rows, :] += jnp.dot(
                e.astype(jnp.bfloat16), un, preferred_element_type=jnp.float32
            )
            dk_acc[rows, :] += jnp.dot(ds, q, preferred_element_type=jnp.float32)
            return dq_sum + contract_rows(k, ds)

        steps = k_ref.shape[1] // chunk
        dq_t = lax.fori_loop(0, steps, keys_step, dq_t, unroll=steps <= 2)

        @pl.when(last)
        def _():
            dk_ref[0] = dk_acc[...].astype(jnp.bfloat16)
            dv_ref[0] = dv_acc[...].astype(jnp.bfloat16)

    dq_ref[0] = jnp.transpose(dq_t).astype(jnp.bfloat16)


def attend_back(q, o, g, own, far, block, head):
    seqs, rows, wide = q.shape
    heads = wide // LANES
    distant = far.shape[1]
    chunk = math.gcd(rows, 1024)
    keys = rows + distant
    own_k = pl.BlockSpec((1, rows, LANES), lambda s, i: (s, 0, head))
    own_v = pl.BlockSpec((1, rows, LANES), lambda s, i: (s, 0, heads + head))
    far_k = pl.BlockSpec((1, distant, LANES), lambda s, i: (s, 0, head))
    far_v = pl.BlockSpec((1, distant, LANES), lambda s, i: (s, 0, heads + head))
    rowwise = pl.BlockSpec((1, block, LANES), lambda s, i: (s, i, head))
    near_out = pl.BlockSpec((1, rows, LANES), lambda s, i: (s, 0, 0))
    far_out = pl.BlockSpec((1, distant, LANES), lambda s, i: (s, 0, 0))
    near_shape = jax.ShapeDtypeStruct((seqs, rows, LANES), jnp.bfloat16)
    far_shape = jax.ShapeDtypeStruct((seqs, distant, LANES), jnp.bfloat16)
    return pl.pallas_call(
        functools.partial(backward_kernel, head=head, chunk=chunk),
        grid=(seqs, rows // block),
        in_specs=[
            rowwise,
            rowwise,
            pl.BlockSpec((1, block, heads * HD), lambda s, i: (s, i, 0)),
            own_k,
            own_v,
            far_k,
            far_v,
        ],
        out_specs=[
            pl.BlockSpec((1, block, LANES), lambda s, i: (s, i, 0)),
            near_out,
            near_out,
            far_out,
            far_out,
        ],
        out_shape=[near_shape, near_shape, near_shape, far_shape, far_shape],
        scratch_shapes=[
            pltpu.VMEM((rows, LANES), jnp.float32),
            pltpu.VMEM((rows, LANES), jnp.float32),
            pltpu.VMEM((distant, LANES), jnp.float32),
            pltpu.VMEM((distant, LANES), jnp.float32),
        ],
        cost_estimate=pl.CostEstimate(
            flops=seqs * rows * keys * 1280,
            transcendentals=seqs * rows * keys,
            bytes_accessed=seqs * (rows + keys) * 1536,
        ),
    )(q, o, g, own, own, far, far)


def pick(stack, index):
    return lax.dynamic_index_in_dim(stack, index, 0, keepdims=False)


def body(
    inputs,
    lengths,
    cotangent,
    query_key_value,
    query_bias,
    value_bias,
    output_weight,
    output_bias,
    first_gain,
    first_shift,
    hidden_weight,
    hidden_bias,
    down_weight,
    down_bias,
    second_gain,
    second_shift,
):
    f32, bf16 = jnp.float32, jnp.bfloat16
    seqs, span, width = inputs.shape
    shards = lax.axis_size("fsdp")
    peers = lax.axis_size("ctx")
    groups = math.gcd(H, peers)
    copies = peers // groups
    planes = peers // 2
    heads = H // groups
    cols = heads * HD
    own_rows = query_key_value.shape[0]
    fsdp = lax.axis_index("fsdp")
    ctx = lax.axis_index("ctx")
    group, copy = ctx // copies, ctx % copies
    plane, core = ctx // 2, ctx % 2
    toks = seqs * span
    rows = groups * span
    ff = hidden_weight.shape[1]

    def move(value, axis, target):
        return lax.ppermute(
            value, axis, [(i, target(i)) for i in range(lax.axis_size(axis))]
        )

    def swap(value):
        return move(value, "ctx", lambda i: i ^ 1)

    def across(value, k):
        return move(value, "fsdp", lambda i: i ^ k)

    def to_group(value, d):
        return move(
            value, "ctx", lambda i: (i // copies + d) % groups * copies + i % copies
        )

    def to_copy(value, d):
        return move(
            value, "ctx", lambda i: i // copies * copies + (i % copies + d) % copies
        )

    def to_plane(value, d):
        return move(value, "ctx", lambda i: (i // 2 + d) % planes * 2 + i % 2)

    def gather_rows(shard):
        pieces = jnp.stack([shard] + [across(shard, k) for k in range(1, shards)])
        return jnp.concatenate([pick(pieces, fsdp ^ g) for g in range(shards)], axis=0)

    def near_pieces(shard):
        half = shard.shape[0] // 2
        mine = lax.dynamic_slice_in_dim(shard, core * half, half, 0)
        return [mine] + [across(mine, k) for k in range(1, shards)]

    def finish_weight(shard, near):
        half = shard.shape[0] // 2
        other = lax.dynamic_slice_in_dim(shard, (1 - core) * half, half, 0)
        far = [other] + [swap(piece) for piece in near[1:]]
        pieces = jnp.stack(near + far)
        ordered = []
        for g in range(shards):
            for side in range(2):
                ordered.append(pick(pieces, jnp.where(core == side, 0, shards) + (fsdp ^ g)))
        return jnp.concatenate(ordered, axis=0)

    x_parts = [inputs] + [to_group(inputs, d) for d in range(1, groups)]

    own_cols = jnp.concatenate(
        [
            lax.dynamic_slice_in_dim(query_key_value, i * width + group * cols, cols, 1)
            for i in range(3)
        ],
        axis=1,
    )
    w_joint = gather_rows(own_cols).reshape(width, 3 * heads, HD)
    scale = jnp.where(jnp.arange(3 * heads) < heads, HD**-0.5, 1.0).astype(bf16)
    w_wide = jnp.pad(w_joint * scale[:, None], ((0, 0), (0, 0), (0, LANES - HD)))
    w_wide = w_wide.reshape(width, 3 * heads * LANES)

    w_output = gather_rows(output_weight)
    near_hidden = near_pieces(hidden_weight)
    near_down = near_pieces(down_weight)

    vectors = (
        query_bias,
        value_bias,
        output_bias,
        first_gain,
        first_shift,
        down_bias,
        second_gain,
        second_shift,
        hidden_bias,
    )
    vectors = lax.optimization_barrier(vectors + (x_parts[1],))
    x_parts[1] = vectors[9]
    packed = jnp.concatenate(
        [jnp.stack(vectors[:8]), vectors[8].reshape(-1, own_rows)], axis=0
    )
    packed = gather_rows(packed[None]).astype(f32)
    b_query, b_value, b_output, g_first, s_first, b_down, g_second, s_second = [
        packed[:, i].reshape(width) for i in range(8)
    ]
    b_hidden = packed[:, 8:].reshape(ff)

    x_all = jnp.concatenate(x_parts, axis=1).reshape(seqs * rows, width)

    place = jnp.stack(
        [(((group - d) % groups) * copies + copy) * span for d in range(groups)]
    )
    place = (place[:, None] + jnp.arange(span, dtype=jnp.int32)).reshape(rows)
    mask = jnp.where(place[None, :] < lengths[:, None], 0.0, MASKED).reshape(seqs * rows, 1)

    def wide_bias(value, ones):
        value = value.reshape(heads, HD)
        tail = jnp.zeros((LANES - HD,), f32).at[jnp.array(ones)].set(1.0)
        return jnp.concatenate(
            [value, jnp.broadcast_to(tail, (heads, LANES - HD))], axis=-1
        ).reshape(heads * LANES)

    wide = heads * LANES
    bias_q = wide_bias(
        lax.dynamic_slice_in_dim(b_query, group * cols, cols) * HD**-0.5, (0,)
    )
    bias_k = wide_bias(jnp.zeros((cols,), f32), (1, 2, 3))
    bias_v = wide_bias(lax.dynamic_slice_in_dim(b_value, group * cols, cols), (0, 1, 2))
    column = jnp.arange(2 * wide)
    masked = jnp.where((column < wide) & (column % LANES == HD), 1.0, 0.0)
    kv_own = (
        jnp.dot(x_all, w_wide[:, wide:], preferred_element_type=f32)
        + jnp.concatenate([bias_k, bias_v])
        + mask * masked
    ).astype(bf16)
    kv_own = kv_own.reshape(seqs, rows, 2 * wide)
    kv_far = [to_copy(kv_own, d) for d in range(1, copies)]
    kv_far = kv_far[0] if copies == 2 else jnp.concatenate(kv_far, axis=1)
    q_wide = (jnp.dot(x_all, w_wide[:, :wide], preferred_element_type=f32) + bias_q).astype(bf16)
    q_wide = q_wide.reshape(seqs, rows, wide)

    block = math.gcd(rows, 256)
    att_low, o_wide, q_wide = attend(q_wide, kv_own, kv_far, block)

    att_low, near_hidden, near_down = lax.optimization_barrier(
        (att_low, near_hidden, near_down)
    )
    att_low = att_low.reshape(seqs, groups, span, cols)
    got = jnp.stack(
        [att_low[:, 0]] + [to_group(att_low[:, d], -d) for d in range(1, groups)]
    )
    w_hidden = finish_weight(hidden_weight, near_hidden)
    w_down = finish_weight(down_weight, near_down)
    attention_low = jnp.concatenate(
        [pick(got, (j - group) % groups) for j in range(groups)], axis=-1
    ).reshape(toks, width)

    tokens = inputs.reshape(toks, width).astype(f32)
    branch = jnp.dot(attention_low, w_output, preferred_element_type=f32) + b_output
    first_out, first_scaled, first_inv = layer_norm(tokens + branch, g_first, s_first)
    first_low = first_out.astype(bf16)
    pre_act = jnp.dot(first_low, w_hidden, preferred_element_type=f32) + b_hidden
    activated = gelu_exact(pre_act).astype(bf16)
    down_out = jnp.dot(activated, w_down, preferred_element_type=f32) + b_down
    second_out, second_scaled, second_inv = layer_norm(first_out + down_out, g_second, s_second)
    outputs = second_out.astype(bf16).reshape(seqs, span, width)
    out_grad = cotangent.reshape(toks, width).astype(f32)
    grad_second_gain = jnp.sum(out_grad * second_scaled, axis=0)
    grad_second_shift = jnp.sum(out_grad, axis=0)
    d_second = norm_grad(out_grad, second_scaled, second_inv, g_second)
    down_back = d_second.astype(bf16)
    grad_down_bias = jnp.sum(down_back.astype(f32), axis=0)
    act_grad = contract_cols(down_back, w_down)
    pre_back = jax.vjp(gelu_exact, pre_act)[1](act_grad)[0].astype(bf16)
    grad_hidden_bias = jnp.sum(pre_back.astype(f32), axis=0)
    d_first = contract_cols(pre_back, w_hidden) + d_second
    grad_first_gain = jnp.sum(d_first * first_scaled, axis=0)
    grad_first_shift = jnp.sum(d_first, axis=0)
    d_first_sum = norm_grad(d_first, first_scaled, first_inv, g_first)
    branch_back = d_first_sum.astype(bf16)
    grad_output_bias = jnp.sum(branch_back.astype(f32), axis=0)
    attention_back = contract_cols(branch_back, w_output).astype(bf16)

    parts = attention_back.reshape(seqs, span, groups, cols).transpose(2, 0, 1, 3)
    g_all = jnp.concatenate(
        [pick(parts, group)]
        + [to_group(pick(parts, (group + d) % groups), d) for d in range(1, groups)],
        axis=1,
    )

    grad_down = contract_rows(activated, down_back).astype(bf16)
    grad_hidden = contract_rows(first_low, pre_back).astype(bf16)
    grad_output = contract_rows(attention_low, branch_back).astype(bf16)

    def reduce_pair(grad):
        half = grad.shape[1] // 2
        grad = grad.reshape(shards, 2, half, -1).transpose(1, 0, 2, 3)
        got = swap(pick(grad, 1 - core))
        return (pick(grad, core).astype(f32) + got.astype(f32)).astype(bf16)

    bits = shards.bit_length() - 1

    def reversed_bits(t):
        return sum(((t >> j) & 1) << (bits - 1 - j) for j in range(bits))

    def hyper(value, j):
        pairs = []
        for f in range(shards):
            for c in range(peers):
                bit = j if c % 2 == 0 else bits - 1 - j
                pairs.append((f * peers + c, (f ^ (1 << bit)) * peers + c))
        return lax.ppermute(value, ("fsdp", "ctx"), pairs)

    def reduce_shards(grad):
        held = {
            t: pick(grad, fsdp ^ jnp.where(core == 0, t, reversed_bits(t)))
            for t in range(shards)
        }
        for j in range(bits):
            sent = [t for t in held if (t >> j) & 1]
            got = hyper(jnp.stack([held.pop(t) for t in sent]), j)
            for i, t in enumerate(sent):
                kept = t ^ (1 << j)
                held[kept] = (held[kept].astype(f32) + got[i].astype(f32)).astype(bf16)
        return held[0]

    def reduce_planes(grad):
        pieces = grad.reshape(planes, grad.shape[0] // planes, -1)
        total = pick(pieces, plane).astype(f32)
        for d in range(1, planes):
            total = total + to_plane(pick(pieces, (plane + d) % planes), d).astype(f32)
        total = total.astype(bf16)
        got = jnp.stack([total] + [to_plane(total, d) for d in range(1, planes)])
        return jnp.concatenate([pick(got, (plane - j) % planes) for j in range(planes)], axis=0)

    def join_pair(half):
        both = jnp.stack([half, swap(half)])
        return jnp.concatenate([pick(both, core), pick(both, 1 - core)], axis=0)

    def reduce_all(grad):
        half = reduce_shards(reduce_pair(grad))
        return join_pair(reduce_planes(half)).astype(f32)

    small = jnp.stack(
        [
            grad_output_bias,
            grad_first_gain,
            grad_first_shift,
            grad_down_bias,
            grad_second_gain,
            grad_second_shift,
        ]
    ).reshape(6, shards, own_rows)
    small = jnp.concatenate(
        [small, grad_hidden_bias.reshape(shards, -1, own_rows).transpose(1, 0, 2)], axis=0
    )
    small_count = small.shape[0] * own_rows
    small = small.transpose(1, 0, 2).reshape(shards, small_count).astype(bf16)
    pad_rows = 64
    small = jnp.pad(small, ((0, 0), (0, pad_rows * width - small_count)))
    small = small.reshape(shards, pad_rows, width)
    total_down = reduce_all(grad_down.reshape(shards, ff // shards, width))
    total_hidden = reduce_all(grad_hidden.reshape(shards, own_rows, ff))
    total_rest = reduce_all(
        jnp.concatenate([grad_output.reshape(shards, own_rows, width), small], axis=1),
    )
    total_output = total_rest[:own_rows]
    flat = total_rest[own_rows:].reshape(-1)[:small_count].reshape(-1, own_rows)

    q_back, k_back, v_back = [], [], []
    for h in range(heads):
        dq, dk, dv, dk_far, dv_far = attend_back(q_wide, o_wide, g_all, kv_own, kv_far, block, h)
        q_back.append(dq)
        for parts, near, far in ((k_back, dk, dk_far), (v_back, dv, dv_far)):
            total = near.astype(f32)
            for d in range(1, copies):
                total = total + to_copy(far[:, (d - 1) * rows : d * rows], -d).astype(f32)
            parts.append(total.astype(bf16))
    joint_back = jnp.concatenate(q_back + k_back + v_back, axis=-1).reshape(seqs * rows, -1)

    partial = contract_cols(joint_back, w_wide).astype(bf16).reshape(seqs, groups, span, width)
    input_grad = partial[:, 0].astype(f32) + d_first_sum.reshape(seqs, span, width)
    for d in range(1, groups):
        input_grad = input_grad + to_group(partial[:, d], -d).astype(f32)

    unscale = jnp.where(jnp.arange(3 * heads) < heads, HD**-0.5, 1.0)[:, None]
    grad_joint = contract_rows(x_all, joint_back).reshape(width, 3 * heads, LANES)
    grad_joint = (grad_joint[..., :HD] * unscale).astype(bf16).reshape(shards, own_rows, -1)
    sums = jnp.sum(joint_back.astype(f32), axis=0).reshape(3 * heads, LANES)[:, :HD] * unscale
    sums = sums.reshape(3, cols)
    tail = jnp.zeros((2, width), f32)
    tail = lax.dynamic_update_slice(tail, sums[::2], (0, group * cols))
    tail = tail.reshape(2, shards, own_rows).transpose(1, 0, 2).reshape(shards, 1, -1)
    extra = 32
    tail = jnp.pad(
        tail.astype(bf16), ((0, 0), (0, extra - 1), (0, 3 * cols - tail.shape[-1]))
    )
    grad_joint = jnp.concatenate([grad_joint, tail], axis=1)
    half = reduce_shards(reduce_pair(grad_joint))
    if copies > 2:
        total = half.astype(f32)
        for d in range(2, copies, 2):
            total = total + to_copy(half, d).astype(f32)
        half = total.astype(bf16)
    got = jnp.stack([half] + [to_group(half, d) for d in range(1, groups)])
    got = join_pair(got.transpose(1, 0, 2).reshape(half.shape[0], -1))
    got = got.reshape(own_rows + extra, groups, 3, cols).astype(f32)
    total_joint = jnp.stack(
        [
            lax.dynamic_index_in_dim(got, (group - j) % groups, 1, keepdims=False)
            for j in range(groups)
        ],
        axis=2,
    )[:own_rows].reshape(own_rows, 3 * width)
    biases = jnp.sum(got[own_rows].reshape(groups, -1), axis=0)

    return (
        outputs,
        input_grad,
        total_joint,
        biases[:own_rows],
        biases[own_rows : 2 * own_rows],
        total_output,
        flat[0],
        flat[1],
        flat[2],
        total_hidden,
        flat[6:].reshape(-1),
        total_down,
        flat[3],
        flat[4],
        flat[5],
    )


def solution(mesh):
    placed = (
        P("fsdp", "ctx", None),
        P("fsdp"),
        P("fsdp", "ctx", None),
        P("fsdp", None),
        P("fsdp"),
        P("fsdp"),
        P("fsdp", None),
        P("fsdp"),
        P("fsdp"),
        P("fsdp"),
        P("fsdp", None),
        P("fsdp"),
        P("fsdp", None),
        P("fsdp"),
        P("fsdp"),
        P("fsdp"),
    )

    return jax.shard_map(
        body,
        mesh=mesh,
        in_specs=placed,
        out_specs=(
            P("fsdp", "ctx", None),
            P("fsdp", "ctx", None),
            P("fsdp", None),
            P("fsdp"),
            P("fsdp"),
            P("fsdp", None),
            P("fsdp"),
            P("fsdp"),
            P("fsdp"),
            P("fsdp", None),
            P("fsdp"),
            P("fsdp", None),
            P("fsdp"),
            P("fsdp"),
            P("fsdp"),
        ),
        check_vma=False,
    )
```

profile of v0, /device:TPU:0, one launch (start us, length us, event | category | flops | bytes accessed | tf_op | source)
XLA Modules:
  0.0 440.3 jit_solution(2401309149568835930)
XLA Ops:
  16.4 3.5 collective-permute-done.5
  21.1 8.9 %collective-permute-done = bf16[1,256,768]{2,1,0:T(8,128)(2,1)S(1)} collective-permute-done((bf16[1,256,768]{2,1,0:T(8,128)(2,1)}, bf16[1,256,768]{2,1,0:T(8,128)(2,1)S(1)}, u32[]{:S(2)}, u32[]{:S(2)}) %collective-permute-start) | collective-permute-done | bytes 393248 | tf_op jit(solution)/shard_map/ppermute | solution.py:282
  41.2 4.0 fusion.20.own_ref.k_own.v_own
  57.0 5.9 %collective-permute-done.21 = bf16[192,768]{1,0:T(8,128)(2,1)} collective-permute-done((bf16[192,768]{1,0:T(8,128)(2,1)}, bf16[192,768]{1,0:T(8,128)(2,1)}, u32[]{:S(2)}, u32[]{:S(2)}) %collective-permute-start.21) | collective-permute-done | bytes 294944 | tf_op jit(solution)/shard_map/ppermute | solution.py:282
  64.4 13.1 %collective-permute-done.20 = bf16[192,768]{1,0:T(8,128)(2,1)} collective-permute-done((bf16[192,768]{1,0:T(8,128)(2,1)}, bf16[192,768]{1,0:T(8,128)(2,1)}, u32[]{:S(2)}, u32[]{:S(2)}) %collective-permute-start.20) | collective-permute-done | bytes 294944 | tf_op jit(solution)/shard_map/ppermute | solution.py:282
  87.6 13.1 %shard_map.298 = (bf16[1,1024,192]{2,1,0:T(8,128)(2,1)}, f32[1,1024,384]{2,1,0:T(8,128)}, bf16[1,1024,384]{2,1,0:T(8,128)(2,1)}) custom-call(bf16[1,1024,384]{2,1,0:T(8,128)(2,1)} %fusion.27.q_ref, bf16[1,1024,768]{2,1,0:T(8,128)(2,1)} %fusion.20.own_ref.k_own.v_own, bf16[1,1024,768]{2,1,0:T(8,128)(2,1)} %collective-permute-done.9.far_ref.k_far.v_far), custom_call_target="tpu_custom_call" | custom-call | flops 3221225472 | bytes 9437184 | tf_op jit(solution)/shard_map/pallas_call | solution.py:96
  102.7 11.6 %collective-permute-done.11 = bf16[96,3072]{1,0:T(8,128)(2,1)} collective-permute-done((bf16[96,3072]{1,0:T(8,128)(2,1)S(1)}, bf16[96,3072]{1,0:T(8,128)(2,1)}, u32[]{:S(2)}, u32[]{:S(2)}) %collective-permute-start.11) | collective-permute-done | bytes 589856 | tf_op jit(solution)/shard_map/ppermute | solution.py:282
  115.5 10.9 %collective-permute-start.18 = (bf16[1,256,192]{2,1,0:T(8,128)(2,1)S(1)}, bf16[1,256,192]{2,1,0:T(8,128)(2,1)S(1)}, u32[]{:S(2)}, u32[]{:S(2)}) collective-permute-start(bf16[1,256,192]{2,1,0:T(8,128)(2,1)S(1)} %get-tuple-element.193), channel_id=1, source_target_pairs={{0,2},{1,3},{2,4},{3,5},{4,6},{5,7},{6,0},{7,1},{8,10},{9,11},{10,... | collective-permute-start | bytes 294920 | tf_op jit(solution)/shard_map/ppermute | solution.py:282
  145.3 8.1 %multiply_convert_fusion = (bf16[256,3072]{1,0:T(8,128)(2,1)S(1)}, f32[256,3072]{1,0:T(8,128)S(1)}, f32[256,3072]{1,0:T(8,128)S(1)}) fusion(f32[3072]{0:T(1024)S(1)} %add.671, bf16[768,3072]{1,0:T(8,128)(2,1)S(1)} %bitcast_dynamic-update-slice_fusion.16, f32[256,768]{1,0:T(8,128)S(1)} %get-tuple-element.226, f32[768]{0:T(1024)S(1)} %add.651, ...), kind=kOutput, calls=%fused_computation.12 | convolution fusion | flops 1260847104 | bytes 13389824 | tf_op jit(solution)/shard_map/dot_general | solution.py:419
  162.4 3.7 convolution_convert_fusion.1
  166.2 3.7 convolution_convert_fusion
  186.0 11.7 %shard_map.300 = (bf16[1,1024,128]{2,1,0:T(8,128)(2,1)}, bf16[1,1024,128]{2,1,0:T(8,128)(2,1)}, bf16[1,1024,128]{2,1,0:T(8,128)(2,1)}, bf16[1,1024,128]{2,1,0:T(8,128)(2,1)}, bf16[1,1024,128]{2,1,0:T(8,128)(2,1)}) custom-call(bf16[1,1024,384]{2,1,0:T(8,128)(2,1)} %get-tuple-element.84.q_ref, f32[1,1024,384]{2,1,0:T(8,128)} %get-tuple-element.85.o_ref, ...), custom_call_target="tpu_custom_call" | custom-call | flops 2684354560 | bytes 4718592 | tf_op jit(solution)/shard_map/pallas_call | solution.py:207
  197.8 11.4 %shard_map.299 = (bf16[1,1024,128]{2,1,0:T(8,128)(2,1)}, bf16[1,1024,128]{2,1,0:T(8,128)(2,1)}, bf16[1,1024,128]{2,1,0:T(8,128)(2,1)}, bf16[1,1024,128]{2,1,0:T(8,128)(2,1)}, bf16[1,1024,128]{2,1,0:T(8,128)(2,1)}) custom-call(bf16[1,1024,384]{2,1,0:T(8,128)(2,1)} %get-tuple-element.84.q_ref, f32[1,1024,384]{2,1,0:T(8,128)} %get-tuple-element.85.o_ref, ...), custom_call_target="tpu_custom_call" | custom-call | flops 2684354560 | bytes 4718592 | tf_op jit(solution)/shard_map/pallas_call | solution.py:207
  209.7 11.3 %shard_map.301 = (bf16[1,1024,128]{2,1,0:T(8,128)(2,1)}, bf16[1,1024,128]{2,1,0:T(8,128)(2,1)}, bf16[1,1024,128]{2,1,0:T(8,128)(2,1)}, bf16[1,1024,128]{2,1,0:T(8,128)(2,1)}, bf16[1,1024,128]{2,1,0:T(8,128)(2,1)}) custom-call(bf16[1,1024,384]{2,1,0:T(8,128)(2,1)} %get-tuple-element.84.q_ref, f32[1,1024,384]{2,1,0:T(8,128)} %get-tuple-element.85.o_ref, ...), custom_call_target="tpu_custom_call" | custom-call | flops 2684354560 | bytes 4718592 | tf_op jit(solution)/shard_map/pallas_call | solution.py:207
  232.6 3.8 multiply_convert_fusion.1
  236.4 3.8 reshape.425
  254.2 3.9 collective-permute-done.48
  260.3 5.6 %collective-permute-done.49 = bf16[1,128,768]{2,1,0:T(8,128)(2,1)S(1)} collective-permute-done((bf16[1,128,768]{2,1,0:T(8,128)(2,1)S(1)}, bf16[1,128,768]{2,1,0:T(8,128)(2,1)S(1)}, u32[]{:S(2)}, u32[]{:S(2)}) %collective-permute-start.49) | collective-permute-done | bytes 196640 | tf_op jit(solution)/shard_map/ppermute | solution.py:469
  284.5 4.1 collective-permute-start.38
  289.6 6.9 %collective-permute-done.37 = bf16[1,256,768]{2,1,0:T(8,128)(2,1)S(1)} collective-permute-done((bf16[1,256,768]{2,1,0:T(8,128)(2,1)S(1)}, bf16[1,256,768]{2,1,0:T(8,128)(2,1)S(1)}, u32[]{:S(2)}, u32[]{:S(2)}) %collective-permute-start.37) | collective-permute-done | bytes 393248 | tf_op jit(solution)/shard_map/ppermute | solution.py:282
  296.8 4.6 %collective-permute-done.39 = bf16[1,256,768]{2,1,0:T(8,128)(2,1)S(1)} collective-permute-done((bf16[1,256,768]{2,1,0:T(8,128)(2,1)S(1)}, bf16[1,256,768]{2,1,0:T(8,128)(2,1)S(1)}, u32[]{:S(2)}, u32[]{:S(2)}) %collective-permute-start.39) | collective-permute-done | bytes 393248 | tf_op jit(solution)/shard_map/ppermute | solution.py:282
  301.4 12.2 %collective-permute-start.44 = (bf16[112,576]{1,0:T(8,128)(2,1)S(1)}, bf16[112,576]{1,0:T(8,128)(2,1)S(1)}, u32[]{:S(2)}, u32[]{:S(2)}) collective-permute-start(bf16[112,576]{1,0:T(8,128)(2,1)S(1)} %bitcast.393), channel_id=1, source_target_pairs={{0,4},{1,5},{2,6},{3,7},{4,0},{5,1},{6,2},{7,3},{8,12},{9,13},{10,... | collective-permute-start | bytes 387080 | tf_op jit(solution)/shard_map/ppermute | solution.py:282
  313.7 7.5 %collective-permute-done.38 = bf16[1,256,768]{2,1,0:T(8,128)(2,1)S(1)} collective-permute-done((bf16[1,256,768]{2,1,0:T(8,128)(2,1)S(1)}, bf16[1,256,768]{2,1,0:T(8,128)(2,1)S(1)}, u32[]{:S(2)}, u32[]{:S(2)}) %collective-permute-start.38) | collective-permute-done | bytes 393248 | tf_op jit(solution)/shard_map/ppermute | solution.py:282
  353.7 17.1 %collective-permute-done.58 = bf16[2,96,3072]{2,1,0:T(8,128)(2,1)} collective-permute-done((bf16[2,96,3072]{2,1,0:T(8,128)(2,1)}, bf16[2,96,3072]{2,1,0:T(8,128)(2,1)}, u32[]{:S(2)}, u32[]{:S(2)}) %collective-permute-start.58) | collective-permute-done | bytes 1179680 | tf_op jit(solution)/shard_map/ppermute | solution.py:469
  375.8 3.8 collective-permute-start.72
  383.4 3.8 collective-permute-start.62
  387.2 9.8 %collective-permute-done.71 = bf16[96,768]{1,0:T(8,128)(2,1)S(1)} collective-permute-done((bf16[96,768]{1,0:T(8,128)(2,1)S(1)}, bf16[96,768]{1,0:T(8,128)(2,1)S(1)}, u32[]{:S(2)}, u32[]{:S(2)}) %collective-permute-start.71) | collective-permute-done | bytes 147488 | tf_op jit(solution)/shard_map/ppermute | solution.py:282
  397.1 5.8 %collective-permute-start.75 = (bf16[96,768]{1,0:T(8,128)(2,1)S(1)}, bf16[96,768]{1,0:T(8,128)(2,1)S(1)}, u32[]{:S(2)}, u32[]{:S(2)}) collective-permute-start(bf16[96,768]{1,0:T(8,128)(2,1)S(1)} %fusion.62), channel_id=1, source_target_pairs={{0,6},{1,7},{2,0},{3,1},{4,2},{5,3},{6,4},{7,5},{8,14},{9,15},{10,... | collective-permute-start | bytes 442376 | tf_op jit(solution)/shard_map/ppermute | solution.py:282
  403.5 11.4 %collective-permute-done.61 = bf16[24,3072]{1,0:T(8,128)(2,1)S(1)} collective-permute-done((bf16[24,3072]{1,0:T(8,128)(2,1)S(1)}, bf16[24,3072]{1,0:T(8,128)(2,1)S(1)}, u32[]{:S(2)}, u32[]{:S(2)}) %collective-permute-start.61) | collective-permute-done | bytes 147488 | tf_op jit(solution)/shard_map/ppermute | solution.py:282
  415.1 3.5 collective-permute-start.63
  418.6 5.8 %collective-permute-done.74 = bf16[96,768]{1,0:T(8,128)(2,1)S(1)} collective-permute-done((bf16[96,768]{1,0:T(8,128)(2,1)S(1)}, bf16[96,768]{1,0:T(8,128)(2,1)S(1)}, u32[]{:S(2)}, u32[]{:S(2)}) %collective-permute-start.74) | collective-permute-done | bytes 147488 | tf_op jit(solution)/shard_map/ppermute | solution.py:282
  425.4 3.9 collective-permute-done.64
  (439 shorter events, 198.6 us)
Async XLA Ops:
  6.9 29.6 %collective-permute-start.1 = (bf16[1,256,768]{2,1,0:T(8,128)(2,1)}, bf16[1,256,768]{2,1,0:T(8,128)(2,1)S(1)}, u32[]{:S(2)}, u32[]{:S(2)}) collective-permute-start(bf16[1,256,768]{2,1,0:T(8,128)(2,1)} %param.21), channel_id=1, source_target_pairs={{0,4},{1,5},{2,6},{3,7},{4,0},{5,1},{6,2},{7,3},{8,12},{9,13},{10,... | collective-permute-start | bytes 1179656 | tf_op jit(solution)/shard_map/ppermute | solution.py:282
  9.9 20.0 %collective-permute-start = (bf16[1,256,768]{2,1,0:T(8,128)(2,1)}, bf16[1,256,768]{2,1,0:T(8,128)(2,1)S(1)}, u32[]{:S(2)}, u32[]{:S(2)}) collective-permute-start(bf16[1,256,768]{2,1,0:T(8,128)(2,1)} %param.21), channel_id=1, source_target_pairs={{0,2},{1,3},{2,4},{3,5},{4,6},{5,7},{6,0},{7,1},{8,10},{9,11},{10,... | collective-permute-start | bytes 1179656 | tf_op jit(solution)/shard_map/ppermute | solution.py:282
  13.8 25.2 %collective-permute-start.2 = (bf16[1,256,768]{2,1,0:T(8,128)(2,1)S(1)}, bf16[1,256,768]{2,1,0:T(8,128)(2,1)}, u32[]{:S(2)}, u32[]{:S(2)}) collective-permute-start(bf16[1,256,768]{2,1,0:T(8,128)(2,1)S(1)} %copy-done.11), channel_id=1, source_target_pairs={{0,6},{1,7},{2,0},{3,1},{4,2},{5,3},{6,4},{7,5},{8,14},{9,15},{10,... | collective-permute-start | bytes 1179656 | tf_op jit(solution)/shard_map/ppermute | solution.py:282
  45.2 37.9 %collective-permute-start.9 = (bf16[1,1024,768]{2,1,0:T(8,128)(2,1)}, bf16[1,1024,768]{2,1,0:T(8,128)(2,1)}, u32[]{:S(2)}, u32[]{:S(2)}) collective-permute-start(bf16[1,1024,768]{2,1,0:T(8,128)(2,1)} %fusion.20.own_ref.k_own.v_own), channel_id=1, source_target_pairs={{0,1},{1,0},{2,3},{3,2},{4,5},{5,4},{6,7},{7,6},{8,9},{9,8},{10,11... | collective-permute-start | bytes 4718600 | tf_op jit(solution)/shard_map/ppermute | solution.py:282
  46.8 16.1 %collective-permute-start.21 = (bf16[192,768]{1,0:T(8,128)(2,1)}, bf16[192,768]{1,0:T(8,128)(2,1)}, u32[]{:S(2)}, u32[]{:S(2)}) collective-permute-start(bf16[192,768]{1,0:T(8,128)(2,1)} %param.27), channel_id=1, source_target_pairs={{0,24},{8,16},{16,8},{24,0},{1,25},{9,17},{17,9},{25,1},{2,26},{10... | collective-permute-start | bytes 884744 | tf_op jit(solution)/shard_map/ppermute | solution.py:282
  48.3 29.2 %collective-permute-start.20 = (bf16[192,768]{1,0:T(8,128)(2,1)}, bf16[192,768]{1,0:T(8,128)(2,1)}, u32[]{:S(2)}, u32[]{:S(2)}) collective-permute-start(bf16[192,768]{1,0:T(8,128)(2,1)} %param.27), channel_id=1, source_target_pairs={{0,16},{8,24},{16,0},{24,8},{1,17},{9,25},{17,1},{25,9},{2,18},{10... | collective-permute-start | bytes 884744 | tf_op jit(solution)/shard_map/ppermute | solution.py:282
  49.8 31.7 %collective-permute-start.15 = (bf16[384,768]{1,0:T(8,128)(2,1)S(1)}, bf16[384,768]{1,0:T(8,128)(2,1)}, u32[]{:S(2)}, u32[]{:S(2)}) collective-permute-start(bf16[384,768]{1,0:T(8,128)(2,1)S(1)} %constant_dynamic-slice_fusion.12), channel_id=1, source_target_pairs={{0,24},{8,16},{16,8},{24,0},{1,25},{9,17},{17,9},{25,1},{2,26},{10... | collective-permute-start | bytes 1769480 | tf_op jit(solution)/shard_map/ppermute | solution.py:282
  55.4 47.3 %collective-permute-start.14 = (bf16[384,768]{1,0:T(8,128)(2,1)S(1)}, bf16[384,768]{1,0:T(8,128)(2,1)}, u32[]{:S(2)}, u32[]{:S(2)}) collective-permute-start(bf16[384,768]{1,0:T(8,128)(2,1)S(1)} %constant_dynamic-slice_fusion.12), channel_id=1, source_target_pairs={{0,16},{8,24},{16,0},{24,8},{1,17},{9,25},{17,1},{25,9},{2,18},{10... | collective-permute-start | bytes 1769480 | tf_op jit(solution)/shard_map/ppermute | solution.py:282
  62.9 39.8 %collective-permute-start.13 = (bf16[384,768]{1,0:T(8,128)(2,1)S(1)}, bf16[384,768]{1,0:T(8,128)(2,1)}, u32[]{:S(2)}, u32[]{:S(2)}) collective-permute-start(bf16[384,768]{1,0:T(8,128)(2,1)S(1)} %constant_dynamic-slice_fusion.12), channel_id=1, source_target_pairs={{0,8},{8,0},{16,24},{24,16},{1,9},{9,1},{17,25},{25,17},{2,10},{10... | collective-permute-start | bytes 1769480 | tf_op jit(solution)/shard_map/ppermute | solution.py:282
  77.4 25.3 %collective-permute-start.12 = (bf16[96,3072]{1,0:T(8,128)(2,1)S(1)}, bf16[96,3072]{1,0:T(8,128)(2,1)}, u32[]{:S(2)}, u32[]{:S(2)}) collective-permute-start(bf16[96,3072]{1,0:T(8,128)(2,1)S(1)} %constant_dynamic-slice_fusion.13), channel_id=1, source_target_pairs={{0,24},{8,16},{16,8},{24,0},{1,25},{9,17},{17,9},{25,1},{2,26},{10... | collective-permute-start | bytes 1769480 | tf_op jit(solution)/shard_map/ppermute | solution.py:282
  81.5 32.8 %collective-permute-start.11 = (bf16[96,3072]{1,0:T(8,128)(2,1)S(1)}, bf16[96,3072]{1,0:T(8,128)(2,1)}, u32[]{:S(2)}, u32[]{:S(2)}) collective-permute-start(bf16[96,3072]{1,0:T(8,128)(2,1)S(1)} %constant_dynamic-slice_fusion.13), channel_id=1, source_target_pairs={{0,16},{8,24},{16,0},{24,8},{1,17},{9,25},{17,1},{25,9},{2,18},{10... | collective-permute-start | bytes 1769480 | tf_op jit(solution)/shard_map/ppermute | solution.py:282
  83.1 31.2 %collective-permute-start.10 = (bf16[96,3072]{1,0:T(8,128)(2,1)S(1)}, bf16[96,3072]{1,0:T(8,128)(2,1)}, u32[]{:S(2)}, u32[]{:S(2)}) collective-permute-start(bf16[96,3072]{1,0:T(8,128)(2,1)S(1)} %constant_dynamic-slice_fusion.13), channel_id=1, source_target_pairs={{0,8},{8,0},{16,24},{24,16},{1,9},{9,1},{17,25},{25,17},{2,10},{10... | collective-permute-start | bytes 1769480 | tf_op jit(solution)/shard_map/ppermute | solution.py:282
  115.5 23.6 %collective-permute-start.18 = (bf16[1,256,192]{2,1,0:T(8,128)(2,1)S(1)}, bf16[1,256,192]{2,1,0:T(8,128)(2,1)S(1)}, u32[]{:S(2)}, u32[]{:S(2)}) collective-permute-start(bf16[1,256,192]{2,1,0:T(8,128)(2,1)S(1)} %get-tuple-element.193), channel_id=1, source_target_pairs={{0,2},{1,3},{2,4},{3,5},{4,6},{5,7},{6,0},{7,1},{8,10},{9,11},{10,... | collective-permute-start | bytes 294920 | tf_op jit(solution)/shard_map/ppermute | solution.py:282
  180.0 68.5 %collective-permute-start.47 = (bf16[4,128,768]{2,1,0:T(8,128)(2,1)}, bf16[4,128,768]{2,1,0:T(8,128)(2,1)}, u32[]{:S(2)}, u32[]{:S(2)}) collective-permute-start(bf16[4,128,768]{2,1,0:T(8,128)(2,1)} %dynamic-slice_bitcast_fusion.2), channel_id=1, source_target_pairs={{0,1},{1,0},{2,3},{3,2},{4,5},{5,4},{6,7},{7,6},{8,9},{9,8},{10,11... | collective-permute-start | bytes 2359304 | tf_op jit(solution)/shard_map/ppermute | solution.py:282
  183.1 147.3 %collective-permute-start.67 = (bf16[4,384,768]{2,1,0:T(8,128)(2,1)}, bf16[4,384,768]{2,1,0:T(8,128)(2,1)}, u32[]{:S(2)}, u32[]{:S(2)}) collective-permute-start(bf16[4,384,768]{2,1,0:T(8,128)(2,1)} %dynamic-slice_bitcast_fusion), channel_id=1, source_target_pairs={{0,1},{1,0},{2,3},{3,2},{4,5},{5,4},{6,7},{7,6},{8,9},{9,8},{10,11... | collective-permute-start | bytes 7077896 | tf_op jit(solution)/shard_map/ppermute | solution.py:282
  183.7 152.8 %collective-permute-start.57 = (bf16[4,96,3072]{2,1,0:T(8,128)(2,1)}, bf16[4,96,3072]{2,1,0:T(8,128)(2,1)}, u32[]{:S(2)}, u32[]{:S(2)}) collective-permute-start(bf16[4,96,3072]{2,1,0:T(8,128)(2,1)} %dynamic-slice_bitcast_fusion.1), channel_id=1, source_target_pairs={{0,1},{1,0},{2,3},{3,2},{4,5},{5,4},{6,7},{7,6},{8,9},{9,8},{10,11... | collective-permute-start | bytes 7077896 | tf_op jit(solution)/shard_map/ppermute | solution.py:282
  197.8 27.7 %collective-permute-start.32 = (bf16[1,1024,128]{2,1,0:T(8,128)(2,1)}, bf16[1,1024,128]{2,1,0:T(8,128)(2,1)S(1)}, u32[]{:S(2)}, u32[]{:S(2)}) collective-permute-start(bf16[1,1024,128]{2,1,0:T(8,128)(2,1)} %get-tuple-element.92), channel_id=1, source_target_pairs={{0,1},{1,0},{2,3},{3,2},{4,5},{5,4},{6,7},{7,6},{8,9},{9,8},{10,11... | collective-permute-start | bytes 786440 | tf_op jit(solution)/shard_map/ppermute | solution.py:282
  280.3 16.2 %collective-permute-start.37 = (bf16[1,256,768]{2,1,0:T(8,128)(2,1)S(1)}, bf16[1,256,768]{2,1,0:T(8,128)(2,1)S(1)}, u32[]{:S(2)}, u32[]{:S(2)}) collective-permute-start(bf16[1,256,768]{2,1,0:T(8,128)(2,1)S(1)} %get-tuple-element.145), channel_id=1, source_target_pairs={{0,6},{1,7},{2,0},{3,1},{4,2},{5,3},{6,4},{7,5},{8,14},{9,15},{10,... | collective-permute-start | bytes 1179656 | tf_op jit(solution)/shard_map/ppermute | solution.py:282
  283.0 18.5 %collective-permute-start.39 = (bf16[1,256,768]{2,1,0:T(8,128)(2,1)S(1)}, bf16[1,256,768]{2,1,0:T(8,128)(2,1)S(1)}, u32[]{:S(2)}, u32[]{:S(2)}) collective-permute-start(bf16[1,256,768]{2,1,0:T(8,128)(2,1)S(1)} %get-tuple-element.146), channel_id=1, source_target_pairs={{0,2},{1,3},{2,4},{3,5},{4,6},{5,7},{6,0},{7,1},{8,10},{9,11},{10,... | collective-permute-start | bytes 1179656 | tf_op jit(solution)/shard_map/ppermute | solution.py:282
  284.5 36.7 %collective-permute-start.38 = (bf16[1,256,768]{2,1,0:T(8,128)(2,1)S(1)}, bf16[1,256,768]{2,1,0:T(8,128)(2,1)S(1)}, u32[]{:S(2)}, u32[]{:S(2)}) collective-permute-start(bf16[1,256,768]{2,1,0:T(8,128)(2,1)S(1)} %get-tuple-element.147), channel_id=1, source_target_pairs={{0,4},{1,5},{2,6},{3,7},{4,0},{5,1},{6,2},{7,3},{8,12},{9,13},{10,... | collective-permute-start | bytes 1179656 | tf_op jit(solution)/shard_map/ppermute | solution.py:282
  296.5 25.2 %collective-permute-start.45 = (bf16[112,576]{1,0:T(8,128)(2,1)S(1)}, bf16[112,576]{1,0:T(8,128)(2,1)S(1)}, u32[]{:S(2)}, u32[]{:S(2)}) collective-permute-start(bf16[112,576]{1,0:T(8,128)(2,1)S(1)} %bitcast.392), channel_id=1, source_target_pairs={{0,6},{1,7},{2,0},{3,1},{4,2},{5,3},{6,4},{7,5},{8,14},{9,15},{10,... | collective-permute-start | bytes 387080 | tf_op jit(solution)/shard_map/ppermute | solution.py:282
  301.4 24.5 %collective-permute-start.44 = (bf16[112,576]{1,0:T(8,128)(2,1)S(1)}, bf16[112,576]{1,0:T(8,128)(2,1)S(1)}, u32[]{:S(2)}, u32[]{:S(2)}) collective-permute-start(bf16[112,576]{1,0:T(8,128)(2,1)S(1)} %bitcast.393), channel_id=1, source_target_pairs={{0,4},{1,5},{2,6},{3,7},{4,0},{5,1},{6,2},{7,3},{8,12},{9,13},{10,... | collective-permute-start | bytes 387080 | tf_op jit(solution)/shard_map/ppermute | solution.py:282
  335.3 16.5 %collective-permute-start.68 = (bf16[2,384,768]{2,1,0:T(8,128)(2,1)}, bf16[2,384,768]{2,1,0:T(8,128)(2,1)}, u32[]{:S(2)}, u32[]{:S(2)}) collective-permute-start(bf16[2,384,768]{2,1,0:T(8,128)(2,1)} %pad_maximum_fusion.8), channel_id=1, source_target_pairs={{0,8},{1,17},{2,10},{3,19},{4,12},{5,21},{6,14},{7,23},{8,0},{9,25... | collective-permute-start | bytes 3538952 | tf_op jit(solution)/shard_map/ppermute | solution.py:469
  340.3 30.5 %collective-permute-start.58 = (bf16[2,96,3072]{2,1,0:T(8,128)(2,1)}, bf16[2,96,3072]{2,1,0:T(8,128)(2,1)}, u32[]{:S(2)}, u32[]{:S(2)}) collective-permute-start(bf16[2,96,3072]{2,1,0:T(8,128)(2,1)} %pad_maximum_fusion.7), channel_id=1, source_target_pairs={{0,8},{1,17},{2,10},{3,19},{4,12},{5,21},{6,14},{7,23},{8,0},{9,25... | collective-permute-start | bytes 3538952 | tf_op jit(solution)/shard_map/ppermute | solution.py:469
  353.1 21.3 %collective-permute-start.69 = (bf16[1,384,768]{2,1,0:T(8,128)(2,1)S(1)}, bf16[1,384,768]{2,1,0:T(8,128)(2,1)S(1)}, u32[]{:S(2)}, u32[]{:S(2)}) collective-permute-start(bf16[1,384,768]{2,1,0:T(8,128)(2,1)S(1)} %add_convert_fusion.5), channel_id=1, source_target_pairs={{0,16},{1,9},{2,18},{3,11},{4,20},{5,13},{6,22},{7,15},{8,24},{9,1... | collective-permute-start | bytes 1769480 | tf_op jit(solution)/shard_map/ppermute | solution.py:469
  379.6 17.4 %collective-permute-start.71 = (bf16[96,768]{1,0:T(8,128)(2,1)S(1)}, bf16[96,768]{1,0:T(8,128)(2,1)S(1)}, u32[]{:S(2)}, u32[]{:S(2)}) collective-permute-start(bf16[96,768]{1,0:T(8,128)(2,1)S(1)} %get-tuple-element.176), channel_id=1, source_target_pairs={{0,4},{1,5},{2,6},{3,7},{4,0},{5,1},{6,2},{7,3},{8,12},{9,13},{10,... | collective-permute-start | bytes 442376 | tf_op jit(solution)/shard_map/ppermute | solution.py:282
  383.3 19.5 %collective-permute-start.60 = (bf16[24,3072]{1,0:T(8,128)(2,1)S(1)}, bf16[24,3072]{1,0:T(8,128)(2,1)S(1)}, u32[]{:S(2)}, u32[]{:S(2)}) collective-permute-start(bf16[24,3072]{1,0:T(8,128)(2,1)S(1)} %get-tuple-element.183), channel_id=1, source_target_pairs={{0,2},{1,3},{2,4},{3,5},{4,6},{5,7},{6,0},{7,1},{8,10},{9,11},{10,... | collective-permute-start | bytes 442376 | tf_op jit(solution)/shard_map/ppermute | solution.py:282
  383.4 20.1 %collective-permute-start.62 = (bf16[24,3072]{1,0:T(8,128)(2,1)S(1)}, bf16[24,3072]{1,0:T(8,128)(2,1)S(1)}, u32[]{:S(2)}, u32[]{:S(2)}) collective-permute-start(bf16[24,3072]{1,0:T(8,128)(2,1)S(1)} %get-tuple-element.184), channel_id=1, source_target_pairs={{0,6},{1,7},{2,0},{3,1},{4,2},{5,3},{6,4},{7,5},{8,14},{9,15},{10,... | collective-permute-start | bytes 442376 | tf_op jit(solution)/shard_map/ppermute | solution.py:282
  387.2 27.7 %collective-permute-start.61 = (bf16[24,3072]{1,0:T(8,128)(2,1)S(1)}, bf16[24,3072]{1,0:T(8,128)(2,1)S(1)}, u32[]{:S(2)}, u32[]{:S(2)}) collective-permute-start(bf16[24,3072]{1,0:T(8,128)(2,1)S(1)} %get-tuple-element.185), channel_id=1, source_target_pairs={{0,4},{1,5},{2,6},{3,7},{4,0},{5,1},{6,2},{7,3},{8,12},{9,13},{10,... | collective-permute-start | bytes 442376 | tf_op jit(solution)/shard_map/ppermute | solution.py:282
  397.1 18.1 %collective-permute-start.75 = (bf16[96,768]{1,0:T(8,128)(2,1)S(1)}, bf16[96,768]{1,0:T(8,128)(2,1)S(1)}, u32[]{:S(2)}, u32[]{:S(2)}) collective-permute-start(bf16[96,768]{1,0:T(8,128)(2,1)S(1)} %fusion.62), channel_id=1, source_target_pairs={{0,6},{1,7},{2,0},{3,1},{4,2},{5,3},{6,4},{7,5},{8,14},{9,15},{10,... | collective-permute-start | bytes 442376 | tf_op jit(solution)/shard_map/ppermute | solution.py:282
  402.8 21.5 %collective-permute-start.74 = (bf16[96,768]{1,0:T(8,128)(2,1)S(1)}, bf16[96,768]{1,0:T(8,128)(2,1)S(1)}, u32[]{:S(2)}, u32[]{:S(2)}) collective-permute-start(bf16[96,768]{1,0:T(8,128)(2,1)S(1)} %fusion.62), channel_id=1, source_target_pairs={{0,4},{1,5},{2,6},{3,7},{4,0},{5,1},{6,2},{7,3},{8,12},{9,13},{10,... | collective-permute-start | bytes 442376 | tf_op jit(solution)/shard_map/ppermute | solution.py:282
  402.9 21.5 %collective-permute-start.73 = (bf16[96,768]{1,0:T(8,128)(2,1)S(1)}, bf16[96,768]{1,0:T(8,128)(2,1)S(1)}, u32[]{:S(2)}, u32[]{:S(2)}) collective-permute-start(bf16[96,768]{1,0:T(8,128)(2,1)S(1)} %fusion.62), channel_id=1, source_target_pairs={{0,2},{1,3},{2,4},{3,5},{4,6},{5,7},{6,0},{7,1},{8,10},{9,11},{10,... | collective-permute-start | bytes 442376 | tf_op jit(solution)/shard_map/ppermute | solution.py:282
  (86 other events, 727.5 us)
where the time goes:
time: 449 us; the launch traced here: 440 us
  waiting for transfers between devices  149 us (33%)
  starting transfers between devices  104 us (23%)
  local copies, waits for them, and re-layouts  55.3 us (12%)
  Pallas kernels  47.5 us (11%)
  other arithmetic  44.3 us (10%)
  matrix products  36.5 us (8%)
    ppermute x69, waiting for transfers between devices, move(): lax.ppermute(value, axis, [(i, target(i)) for i in range(lax.axis_size(ax...  119 us
    ppermute x69, starting transfers between devices, move(): lax.ppermute(value, axis, [(i, target(i)) for i in range(lax.axis_size(ax...  96.6 us
    pallas_call x3, Pallas kernels, attend_back(): pl.pallas_call(functools.partial(backward_kernel, head=head, chunk=chunk)...  34.4 us
    ppermute x8, waiting for transfers between devices, hyper(): return lax.ppermute(value, ('fsdp', 'ctx'), pairs)  30.8 us
    unnamed x122, local copies, waits for them, and re-layouts  16.5 us
    pallas_call x1, Pallas kernels, attend(): pl.pallas_call(functools.partial(forward_kernel, heads=heads), grid=(seqs...  13.1 us
    dot_general x4, matrix products, contract_rows(): lax.dot_general(left, right, (((0,), (0,)), ((), ())), preferred_element_...  11.9 us
  transfers between devices with their start and end apart: 77, of which 35 were waited for; matrix products, arithmetic and copies ran while one was open for 22% of the time, Pallas kernels for 11%

commit v1 on v0

--- a/solution.py
+++ b/solution.py
@@ -306,15 +306,22 @@
         pieces = jnp.stack([shard] + [across(shard, k) for k in range(1, shards)])
         return jnp.concatenate([pick(pieces, fsdp ^ g) for g in range(shards)], axis=0)
 
-    def near_pieces(shard):
+    def near_pieces(mine):
+        pieces = [mine]
+        for k in range(1, shards):
+            pieces.append(across(mine, k))
+        return pieces
+
+    def own_half(shard):
         half = shard.shape[0] // 2
-        mine = lax.dynamic_slice_in_dim(shard, core * half, half, 0)
-        return [mine] + [across(mine, k) for k in range(1, shards)]
+        return lax.dynamic_slice_in_dim(shard, core * half, half, 0)
 
     def finish_weight(shard, near):
         half = shard.shape[0] // 2
         other = lax.dynamic_slice_in_dim(shard, (1 - core) * half, half, 0)
-        far = [other] + [swap(piece) for piece in near[1:]]
+        far = [other]
+        for piece in near[1:]:
+            far.append(swap(piece))
         pieces = jnp.stack(near + far)
         ordered = []
         for g in range(shards):
@@ -333,12 +340,13 @@
     )
     w_joint = gather_rows(own_cols).reshape(width, 3 * heads, HD)
     scale = jnp.where(jnp.arange(3 * heads) < heads, HD**-0.5, 1.0).astype(bf16)
-    w_wide = jnp.pad(w_joint * scale[:, None], ((0, 0), (0, 0), (0, LANES - HD)))
+    w_joint = w_joint * scale[:, None]
+    w_wide = jnp.pad(w_joint, ((0, 0), (0, 0), (0, LANES - HD)))
     w_wide = w_wide.reshape(width, 3 * heads * LANES)
 
-    w_output = gather_rows(output_weight)
-    near_hidden = near_pieces(hidden_weight)
-    near_down = near_pieces(down_weight)
+    near_output = near_pieces(output_weight)
+    near_hidden = near_pieces(own_half(hidden_weight))
+    near_down = near_pieces(own_half(down_weight))
 
     vectors = (
         query_bias,
@@ -399,13 +407,16 @@
     block = math.gcd(rows, 256)
     att_low, o_wide, q_wide = attend(q_wide, kv_own, kv_far, block)
 
-    att_low, near_hidden, near_down = lax.optimization_barrier(
-        (att_low, near_hidden, near_down)
+    att_low, near_hidden, near_down, near_output = lax.optimization_barrier(
+        (att_low, near_hidden, near_down, near_output)
     )
     att_low = att_low.reshape(seqs, groups, span, cols)
-    got = jnp.stack(
-        [att_low[:, 0]] + [to_group(att_low[:, d], -d) for d in range(1, groups)]
-    )
+    got = [att_low[:, 0]]
+    for d in range(1, groups):
+        got.append(to_group(att_low[:, d], -d))
+    got = jnp.stack(got)
+    pieces = jnp.stack(near_output)
+    w_output = jnp.concatenate([pick(pieces, fsdp ^ g) for g in range(shards)], axis=0)
     w_hidden = finish_weight(hidden_weight, near_hidden)
     w_down = finish_weight(down_weight, near_down)
     attention_low = jnp.concatenate(
@@ -439,11 +450,11 @@
     attention_back = contract_cols(branch_back, w_output).astype(bf16)
 
     parts = attention_back.reshape(seqs, span, groups, cols).transpose(2, 0, 1, 3)
-    g_all = jnp.concatenate(
-        [pick(parts, group)]
-        + [to_group(pick(parts, (group + d) % groups), d) for d in range(1, groups)],
-        axis=1,
-    )
+    g_all = [pick(parts, group)]
+    for d in range(1, groups):
+        sent = pick(parts, (group + d) % groups)
+        g_all.append(to_group(sent, d))
+    g_all = jnp.concatenate(g_all, axis=1)
 
     grad_down = contract_rows(activated, down_back).astype(bf16)
     grad_hidden = contract_rows(first_low, pre_back).astype(bf16)
@@ -485,9 +496,14 @@
         pieces = grad.reshape(planes, grad.shape[0] // planes, -1)
         total = pick(pieces, plane).astype(f32)
         for d in range(1, planes):
-            total = total + to_plane(pick(pieces, (plane + d) % planes), d).astype(f32)
+            sent = pick(pieces, (plane + d) % planes)
+            got = to_plane(sent, d)
+            total = total + got.astype(f32)
         total = total.astype(bf16)
-        got = jnp.stack([total] + [to_plane(total, d) for d in range(1, planes)])
+        got = [total]
+        for d in range(1, planes):
+            got.append(to_plane(total, d))
+        got = jnp.stack(got)
         return jnp.concatenate([pick(got, (plane - j) % planes) for j in range(planes)], axis=0)
 
     def join_pair(half):
@@ -526,25 +542,32 @@
 
     q_back, k_back, v_back = [], [], []
     for h in range(heads):
-        dq, dk, dv, dk_far, dv_far = attend_back(q_wide, o_wide, g_all, kv_own, kv_far, block, h)
+        dq, dk, dv, dk_far, dv_far = attend_back(
+            q_wide, o_wide, g_all, kv_own, kv_far, math.gcd(rows, 1024), h
+        )
+        dq, q_wide = lax.optimization_barrier((dq, q_wide))
         q_back.append(dq)
         for parts, near, far in ((k_back, dk, dk_far), (v_back, dv, dv_far)):
             total = near.astype(f32)
             for d in range(1, copies):
                 total = total + to_copy(far[:, (d - 1) * rows : d * rows], -d).astype(f32)
             parts.append(total.astype(bf16))
-    joint_back = jnp.concatenate(q_back + k_back + v_back, axis=-1).reshape(seqs * rows, -1)
-
-    partial = contract_cols(joint_back, w_wide).astype(bf16).reshape(seqs, groups, span, width)
+    joint_back = jnp.concatenate(
+        [value[..., :HD] for value in q_back + k_back + v_back], axis=-1
+    ).reshape(seqs * rows, 3 * cols)
+
+    partial = contract_cols(joint_back, w_joint.reshape(width, 3 * cols)).astype(bf16)
+    partial = partial.reshape(seqs, groups, span, width)
     input_grad = partial[:, 0].astype(f32) + d_first_sum.reshape(seqs, span, width)
     for d in range(1, groups):
-        input_grad = input_grad + to_group(partial[:, d], -d).astype(f32)
-
-    unscale = jnp.where(jnp.arange(3 * heads) < heads, HD**-0.5, 1.0)[:, None]
-    grad_joint = contract_rows(x_all, joint_back).reshape(width, 3 * heads, LANES)
-    grad_joint = (grad_joint[..., :HD] * unscale).astype(bf16).reshape(shards, own_rows, -1)
-    sums = jnp.sum(joint_back.astype(f32), axis=0).reshape(3 * heads, LANES)[:, :HD] * unscale
-    sums = sums.reshape(3, cols)
+        sent = partial[:, d]
+        sent = to_group(sent, -d)
+        input_grad = input_grad + sent.astype(f32)
+
+    unscale = jnp.repeat(jnp.array([HD**-0.5, 1.0, 1.0], f32), cols)
+    grad_joint = (contract_rows(x_all, joint_back) * unscale).astype(bf16)
+    grad_joint = grad_joint.reshape(shards, own_rows, 3 * cols)
+    sums = (jnp.sum(joint_back.astype(f32), axis=0) * unscale).reshape(3, cols)
     tail = jnp.zeros((2, width), f32)
     tail = lax.dynamic_update_slice(tail, sums[::2], (0, group * cols))
     tail = tail.reshape(2, shards, own_rows).transpose(1, 0, 2).reshape(shards, 1, -1)

time: 449 us -> 430 us (0.958)
  starting transfers between devices: 104 us -> 121 us
  local copies, waits for them, and re-layouts: 55.3 us -> 41 us
  waiting for transfers between devices: 149 us -> 137 us
  Pallas kernels: 47.5 us -> 36.2 us
    ppermute x69, starting transfers between devices: 96.6 us -> 112 us  [move(): lax.ppermute(value, axis, [(i, target(i)) for i in range(lax.axis_size(ax...]
    ppermute x69, waiting for transfers between devices: 119 us -> 106 us  [move(): lax.ppermute(value, axis, [(i, target(i)) for i in range(lax.axis_size(ax...]
    pallas_call x3, Pallas kernels: 34.4 us -> 23.1 us  [attend_back(): pl.pallas_call(functools.partial(backward_kernel, head=head, chunk=chunk)...]
    unnamed x122 -> x112, local copies, waits for them, and re-layouts: 16.5 us -> 10.7 us
    convert_element_type x0 -> x6, other arithmetic: none -> 4.69 us  [body(): parts.append(total.astype(bf16))]
  transfers between devices with their start and end apart: 77 -> 77, of which waited for: 35 -> 33; matrix products, arithmetic and copies ran while one was open for 22% -> 20% of each run, Pallas kernels for 11% -> 9%
where the time goes in v1:
time: 430 us; the launch traced here: 422 us
  waiting for transfers between devices  137 us (32%)
  starting transfers between devices  121 us (28%)
  other arithmetic  46.9 us (11%)
  local copies, waits for them, and re-layouts  41 us (10%)
  matrix products  36.9 us (9%)
  Pallas kernels  36.2 us (8%)
    ppermute x69, starting transfers between devices, move(): lax.ppermute(value, axis, [(i, target(i)) for i in range(lax.axis_size(ax...  112 us
    ppermute x69, waiting for transfers between devices, move(): lax.ppermute(value, axis, [(i, target(i)) for i in range(lax.axis_size(ax...  106 us
    ppermute x8, waiting for transfers between devices, hyper(): return lax.ppermute(value, ('fsdp', 'ctx'), pairs)  30.4 us
    pallas_call x3, Pallas kernels, attend_back(): pl.pallas_call(functools.partial(backward_kernel, head=head, chunk=chunk)...  23.1 us
    pallas_call x1, Pallas kernels, attend(): pl.pallas_call(functools.partial(forward_kernel, heads=heads), grid=(seqs...  13.1 us
    dot_general x4, matrix products, contract_rows(): lax.dot_general(left, right, (((0,), (0,)), ((), ())), preferred_element_...  13 us
    unnamed x112, local copies, waits for them, and re-layouts  10.7 us
    ppermute x8, starting transfers between devices, hyper(): return lax.ppermute(value, ('fsdp', 'ctx'), pairs)  8.98 us
  transfers between devices with their start and end apart: 77, of which 33 were waited for; matrix products, arithmetic and copies ran while one was open for 20% of the time, Pallas kernels for 9%

profile of v1, /device:TPU:0, one launch (start us, length us, event | category | flops | bytes accessed | tf_op | source)
XLA Modules:
  0.0 421.8 jit_solution(2771785817949405949)
XLA Ops:
  20.5 9.6 %collective-permute-done = bf16[1,256,768]{2,1,0:T(8,128)(2,1)S(1)} collective-permute-done((bf16[1,256,768]{2,1,0:T(8,128)(2,1)}, bf16[1,256,768]{2,1,0:T(8,128)(2,1)S(1)}, u32[]{:S(2)}, u32[]{:S(2)}) %collective-permute-start) | collective-permute-done | bytes 393248 | tf_op jit(solution)/shard_map/ppermute | solution.py:282
  39.2 4.0 fusion.10.own_ref.k_own.v_own
  56.5 4.8 %collective-permute-done.18 = bf16[192,768]{1,0:T(8,128)(2,1)} collective-permute-done((bf16[192,768]{1,0:T(8,128)(2,1)}, bf16[192,768]{1,0:T(8,128)(2,1)}, u32[]{:S(2)}, u32[]{:S(2)}) %collective-permute-start.18) | collective-permute-done | bytes 294944 | tf_op jit(solution)/shard_map/ppermute | solution.py:282
  63.8 10.1 %collective-permute-done.15 = bf16[384,768]{1,0:T(8,128)(2,1)} collective-permute-done((bf16[384,768]{1,0:T(8,128)(2,1)S(1)}, bf16[384,768]{1,0:T(8,128)(2,1)}, u32[]{:S(2)}, u32[]{:S(2)}) %collective-permute-start.15) | collective-permute-done | bytes 589856 | tf_op jit(solution)/shard_map/ppermute | solution.py:282
  80.2 13.1 %shard_map.307 = (bf16[1,1024,192]{2,1,0:T(8,128)(2,1)}, f32[1,1024,384]{2,1,0:T(8,128)}, bf16[1,1024,384]{2,1,0:T(8,128)(2,1)}) custom-call(bf16[1,1024,384]{2,1,0:T(8,128)(2,1)} %fusion.13.q_ref, bf16[1,1024,768]{2,1,0:T(8,128)(2,1)} %fusion.10.own_ref.k_own.v_own, bf16[1,1024,768]{2,1,0:T(8,128)(2,1)} %collective-permute-done.9.far_ref.k_far.v_far), custom_call_target="tpu_custom_call" | custom-call | flops 3221225472 | bytes 9437184 | tf_op jit(solution)/shard_map/pallas_call | solution.py:96
  93.4 5.9 %collective-permute-done.12 = bf16[96,3072]{1,0:T(8,128)(2,1)} collective-permute-done((bf16[96,3072]{1,0:T(8,128)(2,1)S(1)}, bf16[96,3072]{1,0:T(8,128)(2,1)}, u32[]{:S(2)}, u32[]{:S(2)}) %collective-permute-start.12) | collective-permute-done | bytes 589856 | tf_op jit(solution)/shard_map/ppermute | solution.py:282
  99.2 11.7 %collective-permute-done.11 = bf16[96,3072]{1,0:T(8,128)(2,1)} collective-permute-done((bf16[96,3072]{1,0:T(8,128)(2,1)S(1)}, bf16[96,3072]{1,0:T(8,128)(2,1)}, u32[]{:S(2)}, u32[]{:S(2)}) %collective-permute-start.11) | collective-permute-done | bytes 589856 | tf_op jit(solution)/shard_map/ppermute | solution.py:282
  112.3 12.8 %collective-permute-start.21 = (bf16[1,256,192]{2,1,0:T(8,128)(2,1)S(1)}, bf16[1,256,192]{2,1,0:T(8,128)(2,1)S(1)}, u32[]{:S(2)}, u32[]{:S(2)}) collective-permute-start(bf16[1,256,192]{2,1,0:T(8,128)(2,1)S(1)} %get-tuple-element.211), channel_id=1, source_target_pairs={{0,2},{1,3},{2,4},{3,5},{4,6},{5,7},{6,0},{7,1},{8,10},{9,11},{10,... | collective-permute-start | bytes 294920 | tf_op jit(solution)/shard_map/ppermute | solution.py:282
  145.4 8.1 %multiply_convert_fusion = (bf16[256,3072]{1,0:T(8,128)(2,1)S(1)}, f32[256,3072]{1,0:T(8,128)S(1)}, f32[256,3072]{1,0:T(8,128)S(1)}) fusion(f32[3072]{0:T(1024)S(1)} %add.671, bf16[768,3072]{1,0:T(8,128)(2,1)S(1)} %bitcast_dynamic-update-slice_fusion.16, f32[256,768]{1,0:T(8,128)S(1)} %get-tuple-element.244, f32[768]{0:T(1024)S(1)} %add.651, ...), kind=kOutput, calls=%fused_computation.11 | convolution fusion | flops 1260847104 | bytes 13389824 | tf_op jit(solution)/shard_map/dot_general | solution.py:430
  186.3 7.6 %shard_map.308 = (bf16[1,1024,128]{2,1,0:T(8,128)(2,1)}, bf16[1,1024,128]{2,1,0:T(8,128)(2,1)}, bf16[1,1024,128]{2,1,0:T(8,128)(2,1)}, bf16[1,1024,128]{2,1,0:T(8,128)(2,1)}, bf16[1,1024,128]{2,1,0:T(8,128)(2,1)}) custom-call(bf16[1,1024,384]{2,1,0:T(8,128)(2,1)} %get-tuple-element.104.q_ref, f32[1,1024,384]{2,1,0:T(8,128)} %get-tuple-element.98.o_ref, ...), custom_call_target="tpu_custom_call" | custom-call | flops 2684354560 | bytes 4718592 | tf_op jit(solution)/shard_map/pallas_call | solution.py:207
  194.4 7.6 %shard_map.309 = (bf16[1,1024,128]{2,1,0:T(8,128)(2,1)}, bf16[1,1024,128]{2,1,0:T(8,128)(2,1)}, bf16[1,1024,128]{2,1,0:T(8,128)(2,1)}, bf16[1,1024,128]{2,1,0:T(8,128)(2,1)}, bf16[1,1024,128]{2,1,0:T(8,128)(2,1)}) custom-call(bf16[1,1024,384]{2,1,0:T(8,128)(2,1)} %get-tuple-element.104.q_ref, f32[1,1024,384]{2,1,0:T(8,128)} %get-tuple-element.98.o_ref, ...), custom_call_target="tpu_custom_call" | custom-call | flops 2684354560 | bytes 4718592 | tf_op jit(solution)/shard_map/pallas_call | solution.py:207
  202.0 7.9 %shard_map.310 = (bf16[1,1024,128]{2,1,0:T(8,128)(2,1)}, bf16[1,1024,128]{2,1,0:T(8,128)(2,1)}, bf16[1,1024,128]{2,1,0:T(8,128)(2,1)}, bf16[1,1024,128]{2,1,0:T(8,128)(2,1)}, bf16[1,1024,128]{2,1,0:T(8,128)(2,1)}) custom-call(bf16[1,1024,384]{2,1,0:T(8,128)(2,1)} %get-tuple-element.104.q_ref, f32[1,1024,384]{2,1,0:T(8,128)} %get-tuple-element.98.o_ref, ...), custom_call_target="tpu_custom_call" | custom-call | flops 2684354560 | bytes 4718592 | tf_op jit(solution)/shard_map/pallas_call | solution.py:207
  222.1 3.9 multiply_convert_fusion.1
  234.0 5.4 %collective-permute-done.48 = bf16[2,128,768]{2,1,0:T(8,128)(2,1)S(1)} collective-permute-done((bf16[2,128,768]{2,1,0:T(8,128)(2,1)S(1)}, bf16[2,128,768]{2,1,0:T(8,128)(2,1)S(1)}, u32[]{:S(2)}, u32[]{:S(2)}) %collective-permute-start.48) | collective-permute-done | bytes 393248 | tf_op jit(solution)/shard_map/ppermute | solution.py:480
  241.6 5.4 %collective-permute-done.49 = bf16[1,128,768]{2,1,0:T(8,128)(2,1)S(1)} collective-permute-done((bf16[1,128,768]{2,1,0:T(8,128)(2,1)S(1)}, bf16[1,128,768]{2,1,0:T(8,128)(2,1)S(1)}, u32[]{:S(2)}, u32[]{:S(2)}) %collective-permute-start.49) | collective-permute-done | bytes 196640 | tf_op jit(solution)/shard_map/ppermute | solution.py:480
  261.4 4.1 collective-permute-start.37
  265.5 4.8 %collective-permute-start.38 = (bf16[1,256,768]{2,1,0:T(8,128)(2,1)}, bf16[1,256,768]{2,1,0:T(8,128)(2,1)S(1)}, u32[]{:S(2)}, u32[]{:S(2)}) collective-permute-start(bf16[1,256,768]{2,1,0:T(8,128)(2,1)} %get-tuple-element.165), channel_id=1, source_target_pairs={{0,4},{1,5},{2,6},{3,7},{4,0},{5,1},{6,2},{7,3},{8,12},{9,13},{10,... | collective-permute-start | bytes 1179656 | tf_op jit(solution)/shard_map/ppermute | solution.py:282
  271.4 7.5 %collective-permute-done.37 = bf16[1,256,768]{2,1,0:T(8,128)(2,1)S(1)} collective-permute-done((bf16[1,256,768]{2,1,0:T(8,128)(2,1)}, bf16[1,256,768]{2,1,0:T(8,128)(2,1)S(1)}, u32[]{:S(2)}, u32[]{:S(2)}) %collective-permute-start.37) | collective-permute-done | bytes 393248 | tf_op jit(solution)/shard_map/ppermute | solution.py:282
  279.7 4.4 %collective-permute-done.39 = bf16[1,256,768]{2,1,0:T(8,128)(2,1)S(1)} collective-permute-done((bf16[1,256,768]{2,1,0:T(8,128)(2,1)}, bf16[1,256,768]{2,1,0:T(8,128)(2,1)S(1)}, u32[]{:S(2)}, u32[]{:S(2)}) %collective-permute-start.39) | collective-permute-done | bytes 393248 | tf_op jit(solution)/shard_map/ppermute | solution.py:282
  284.1 11.5 %collective-permute-start.44 = (bf16[112,576]{1,0:T(8,128)(2,1)S(1)}, bf16[112,576]{1,0:T(8,128)(2,1)S(1)}, u32[]{:S(2)}, u32[]{:S(2)}) collective-permute-start(bf16[112,576]{1,0:T(8,128)(2,1)S(1)} %bitcast.387), channel_id=1, source_target_pairs={{0,4},{1,5},{2,6},{3,7},{4,0},{5,1},{6,2},{7,3},{8,12},{9,13},{10,... | collective-permute-start | bytes 387080 | tf_op jit(solution)/shard_map/ppermute | solution.py:282
  295.6 6.5 %collective-permute-done.38 = bf16[1,256,768]{2,1,0:T(8,128)(2,1)S(1)} collective-permute-done((bf16[1,256,768]{2,1,0:T(8,128)(2,1)}, bf16[1,256,768]{2,1,0:T(8,128)(2,1)S(1)}, u32[]{:S(2)}, u32[]{:S(2)}) %collective-permute-start.38) | collective-permute-done | bytes 393248 | tf_op jit(solution)/shard_map/ppermute | solution.py:282
  305.2 4.6 %collective-permute-done.43 = bf16[112,576]{1,0:T(8,128)(2,1)S(1)} collective-permute-done((bf16[112,576]{1,0:T(8,128)(2,1)S(1)}, bf16[112,576]{1,0:T(8,128)(2,1)S(1)}, u32[]{:S(2)}, u32[]{:S(2)}) %collective-permute-start.43) | collective-permute-done | bytes 129056 | tf_op jit(solution)/shard_map/ppermute | solution.py:282
  337.0 16.3 %collective-permute-done.58 = bf16[2,96,3072]{2,1,0:T(8,128)(2,1)} collective-permute-done((bf16[2,96,3072]{2,1,0:T(8,128)(2,1)}, bf16[2,96,3072]{2,1,0:T(8,128)(2,1)}, u32[]{:S(2)}, u32[]{:S(2)}) %collective-permute-start.58) | collective-permute-done | bytes 1179680 | tf_op jit(solution)/shard_map/ppermute | solution.py:480
  359.1 3.8 collective-permute-start.72
  365.8 3.8 collective-permute-start.62
  370.6 8.1 %collective-permute-done.71 = bf16[96,768]{1,0:T(8,128)(2,1)S(1)} collective-permute-done((bf16[96,768]{1,0:T(8,128)(2,1)S(1)}, bf16[96,768]{1,0:T(8,128)(2,1)S(1)}, u32[]{:S(2)}, u32[]{:S(2)}) %collective-permute-start.71) | collective-permute-done | bytes 147488 | tf_op jit(solution)/shard_map/ppermute | solution.py:282
  378.7 7.1 %collective-permute-start.75 = (bf16[96,768]{1,0:T(8,128)(2,1)S(1)}, bf16[96,768]{1,0:T(8,128)(2,1)S(1)}, u32[]{:S(2)}, u32[]{:S(2)}) collective-permute-start(bf16[96,768]{1,0:T(8,128)(2,1)S(1)} %fusion.52), channel_id=1, source_target_pairs={{0,6},{1,7},{2,0},{3,1},{4,2},{5,3},{6,4},{7,5},{8,14},{9,15},{10,... | collective-permute-start | bytes 442376 | tf_op jit(solution)/shard_map/ppermute | solution.py:282
  386.5 5.1 %collective-permute-done.61 = bf16[24,3072]{1,0:T(8,128)(2,1)S(1)} collective-permute-done((bf16[24,3072]{1,0:T(8,128)(2,1)S(1)}, bf16[24,3072]{1,0:T(8,128)(2,1)S(1)}, u32[]{:S(2)}, u32[]{:S(2)}) %collective-permute-start.61) | collective-permute-done | bytes 147488 | tf_op jit(solution)/shard_map/ppermute | solution.py:282
  391.6 4.3 %collective-permute-start.65 = (bf16[24,3072]{1,0:T(8,128)(2,1)S(1)}, bf16[24,3072]{1,0:T(8,128)(2,1)S(1)}, u32[]{:S(2)}, u32[]{:S(2)}) collective-permute-start(bf16[24,3072]{1,0:T(8,128)(2,1)S(1)} %fusion.55), channel_id=1, source_target_pairs={{0,6},{1,7},{2,0},{3,1},{4,2},{5,3},{6,4},{7,5},{8,14},{9,15},{10,... | collective-permute-start | bytes 442376 | tf_op jit(solution)/shard_map/ppermute | solution.py:282
  396.0 5.5 %collective-permute-start.63 = (bf16[24,3072]{1,0:T(8,128)(2,1)S(1)}, bf16[24,3072]{1,0:T(8,128)(2,1)S(1)}, u32[]{:S(2)}, u32[]{:S(2)}) collective-permute-start(bf16[24,3072]{1,0:T(8,128)(2,1)S(1)} %fusion.55), channel_id=1, source_target_pairs={{0,2},{1,3},{2,4},{3,5},{4,6},{5,7},{6,0},{7,1},{8,10},{9,11},{10,... | collective-permute-start | bytes 442376 | tf_op jit(solution)/shard_map/ppermute | solution.py:282
  401.4 4.2 collective-permute-done.74
  406.7 4.4 %collective-permute-done.64 = bf16[24,3072]{1,0:T(8,128)(2,1)S(1)} collective-permute-done((bf16[24,3072]{1,0:T(8,128)(2,1)S(1)}, bf16[24,3072]{1,0:T(8,128)(2,1)S(1)}, u32[]{:S(2)}, u32[]{:S(2)}) %collective-permute-start.64) | collective-permute-done | bytes 147488 | tf_op jit(solution)/shard_map/ppermute | solution.py:282
  (429 shorter events, 194.6 us)
Async XLA Ops:
  7.0 30.4 %collective-permute-start.1 = (bf16[1,256,768]{2,1,0:T(8,128)(2,1)}, bf16[1,256,768]{2,1,0:T(8,128)(2,1)}, u32[]{:S(2)}, u32[]{:S(2)}) collective-permute-start(bf16[1,256,768]{2,1,0:T(8,128)(2,1)} %param.22), channel_id=1, source_target_pairs={{0,4},{1,5},{2,6},{3,7},{4,0},{5,1},{6,2},{7,3},{8,12},{9,13},{10,... | collective-permute-start | bytes 1179656 | tf_op jit(solution)/shard_map/ppermute | solution.py:282
  10.0 20.1 %collective-permute-start = (bf16[1,256,768]{2,1,0:T(8,128)(2,1)}, bf16[1,256,768]{2,1,0:T(8,128)(2,1)S(1)}, u32[]{:S(2)}, u32[]{:S(2)}) collective-permute-start(bf16[1,256,768]{2,1,0:T(8,128)(2,1)} %param.22), channel_id=1, source_target_pairs={{0,2},{1,3},{2,4},{3,5},{4,6},{5,7},{6,0},{7,1},{8,10},{9,11},{10,... | collective-permute-start | bytes 1179656 | tf_op jit(solution)/shard_map/ppermute | solution.py:282
  13.7 25.5 %collective-permute-start.2 = (bf16[1,256,768]{2,1,0:T(8,128)(2,1)}, bf16[1,256,768]{2,1,0:T(8,128)(2,1)}, u32[]{:S(2)}, u32[]{:S(2)}) collective-permute-start(bf16[1,256,768]{2,1,0:T(8,128)(2,1)} %param.22), channel_id=1, source_target_pairs={{0,6},{1,7},{2,0},{3,1},{4,2},{5,3},{6,4},{7,5},{8,14},{9,15},{10,... | collective-permute-start | bytes 1179656 | tf_op jit(solution)/shard_map/ppermute | solution.py:282
  43.2 32.3 %collective-permute-start.9 = (bf16[1,1024,768]{2,1,0:T(8,128)(2,1)}, bf16[1,1024,768]{2,1,0:T(8,128)(2,1)}, u32[]{:S(2)}, u32[]{:S(2)}) collective-permute-start(bf16[1,1024,768]{2,1,0:T(8,128)(2,1)} %fusion.10.own_ref.k_own.v_own), channel_id=1, source_target_pairs={{0,1},{1,0},{2,3},{3,2},{4,5},{5,4},{6,7},{7,6},{8,9},{9,8},{10,11... | collective-permute-start | bytes 4718600 | tf_op jit(solution)/shard_map/ppermute | solution.py:282
  47.9 26.1 %collective-permute-start.15 = (bf16[384,768]{1,0:T(8,128)(2,1)S(1)}, bf16[384,768]{1,0:T(8,128)(2,1)}, u32[]{:S(2)}, u32[]{:S(2)}) collective-permute-start(bf16[384,768]{1,0:T(8,128)(2,1)S(1)} %constant_dynamic-slice_fusion.12), channel_id=1, source_target_pairs={{0,24},{8,16},{16,8},{24,0},{1,25},{9,17},{17,9},{25,1},{2,26},{10... | collective-permute-start | bytes 1769480 | tf_op jit(solution)/shard_map/ppermute | solution.py:282
  53.2 40.1 %collective-permute-start.14 = (bf16[384,768]{1,0:T(8,128)(2,1)S(1)}, bf16[384,768]{1,0:T(8,128)(2,1)}, u32[]{:S(2)}, u32[]{:S(2)}) collective-permute-start(bf16[384,768]{1,0:T(8,128)(2,1)S(1)} %constant_dynamic-slice_fusion.12), channel_id=1, source_target_pairs={{0,16},{8,24},{16,0},{24,8},{1,17},{9,25},{17,1},{25,9},{2,18},{10... | collective-permute-start | bytes 1769480 | tf_op jit(solution)/shard_map/ppermute | solution.py:282
  55.0 38.3 %collective-permute-start.13 = (bf16[384,768]{1,0:T(8,128)(2,1)S(1)}, bf16[384,768]{1,0:T(8,128)(2,1)}, u32[]{:S(2)}, u32[]{:S(2)}) collective-permute-start(bf16[384,768]{1,0:T(8,128)(2,1)S(1)} %constant_dynamic-slice_fusion.12), channel_id=1, source_target_pairs={{0,8},{8,0},{16,24},{24,16},{1,9},{9,1},{17,25},{25,17},{2,10},{10... | collective-permute-start | bytes 1769480 | tf_op jit(solution)/shard_map/ppermute | solution.py:282
  61.3 37.9 %collective-permute-start.12 = (bf16[96,3072]{1,0:T(8,128)(2,1)S(1)}, bf16[96,3072]{1,0:T(8,128)(2,1)}, u32[]{:S(2)}, u32[]{:S(2)}) collective-permute-start(bf16[96,3072]{1,0:T(8,128)(2,1)S(1)} %constant_dynamic-slice_fusion.13), channel_id=1, source_target_pairs={{0,24},{8,16},{16,8},{24,0},{1,25},{9,17},{17,9},{25,1},{2,26},{10... | collective-permute-start | bytes 1769480 | tf_op jit(solution)/shard_map/ppermute | solution.py:282
  73.9 37.1 %collective-permute-start.11 = (bf16[96,3072]{1,0:T(8,128)(2,1)S(1)}, bf16[96,3072]{1,0:T(8,128)(2,1)}, u32[]{:S(2)}, u32[]{:S(2)}) collective-permute-start(bf16[96,3072]{1,0:T(8,128)(2,1)S(1)} %constant_dynamic-slice_fusion.13), channel_id=1, source_target_pairs={{0,16},{8,24},{16,0},{24,8},{1,17},{9,25},{17,1},{25,9},{2,18},{10... | collective-permute-start | bytes 1769480 | tf_op jit(solution)/shard_map/ppermute | solution.py:282
  75.5 35.7 %collective-permute-start.10 = (bf16[96,3072]{1,0:T(8,128)(2,1)S(1)}, bf16[96,3072]{1,0:T(8,128)(2,1)}, u32[]{:S(2)}, u32[]{:S(2)}) collective-permute-start(bf16[96,3072]{1,0:T(8,128)(2,1)S(1)} %constant_dynamic-slice_fusion.13), channel_id=1, source_target_pairs={{0,8},{8,0},{16,24},{24,16},{1,9},{9,1},{17,25},{25,17},{2,10},{10... | collective-permute-start | bytes 1769480 | tf_op jit(solution)/shard_map/ppermute | solution.py:282
  112.3 26.8 %collective-permute-start.21 = (bf16[1,256,192]{2,1,0:T(8,128)(2,1)S(1)}, bf16[1,256,192]{2,1,0:T(8,128)(2,1)S(1)}, u32[]{:S(2)}, u32[]{:S(2)}) collective-permute-start(bf16[1,256,192]{2,1,0:T(8,128)(2,1)S(1)} %get-tuple-element.211), channel_id=1, source_target_pairs={{0,2},{1,3},{2,4},{3,5},{4,6},{5,7},{6,0},{7,1},{8,10},{9,11},{10,... | collective-permute-start | bytes 294920 | tf_op jit(solution)/shard_map/ppermute | solution.py:282
  179.1 51.1 %collective-permute-start.47 = (bf16[4,128,768]{2,1,0:T(8,128)(2,1)}, bf16[4,128,768]{2,1,0:T(8,128)(2,1)}, u32[]{:S(2)}, u32[]{:S(2)}) collective-permute-start(bf16[4,128,768]{2,1,0:T(8,128)(2,1)} %dynamic-slice_bitcast_fusion.2), channel_id=1, source_target_pairs={{0,1},{1,0},{2,3},{3,2},{4,5},{5,4},{6,7},{7,6},{8,9},{9,8},{10,11... | collective-permute-start | bytes 2359304 | tf_op jit(solution)/shard_map/ppermute | solution.py:282
  182.2 131.0 %collective-permute-start.67 = (bf16[4,384,768]{2,1,0:T(8,128)(2,1)}, bf16[4,384,768]{2,1,0:T(8,128)(2,1)}, u32[]{:S(2)}, u32[]{:S(2)}) collective-permute-start(bf16[4,384,768]{2,1,0:T(8,128)(2,1)} %dynamic-slice_bitcast_fusion), channel_id=1, source_target_pairs={{0,1},{1,0},{2,3},{3,2},{4,5},{5,4},{6,7},{7,6},{8,9},{9,8},{10,11... | collective-permute-start | bytes 7077896 | tf_op jit(solution)/shard_map/ppermute | solution.py:282
  182.7 135.7 %collective-permute-start.57 = (bf16[4,96,3072]{2,1,0:T(8,128)(2,1)}, bf16[4,96,3072]{2,1,0:T(8,128)(2,1)}, u32[]{:S(2)}, u32[]{:S(2)}) collective-permute-start(bf16[4,96,3072]{2,1,0:T(8,128)(2,1)} %dynamic-slice_bitcast_fusion.1), channel_id=1, source_target_pairs={{0,1},{1,0},{2,3},{3,2},{4,5},{5,4},{6,7},{7,6},{8,9},{9,8},{10,11... | collective-permute-start | bytes 7077896 | tf_op jit(solution)/shard_map/ppermute | solution.py:282
  193.9 16.0 %collective-permute-start.31 = (bf16[1,1024,128]{2,1,0:T(8,128)(2,1)}, bf16[1,1024,128]{2,1,0:T(8,128)(2,1)S(1)}, u32[]{:S(2)}, u32[]{:S(2)}) collective-permute-start(bf16[1,1024,128]{2,1,0:T(8,128)(2,1)} %get-tuple-element.108), channel_id=1, source_target_pairs={{0,1},{1,0},{2,3},{3,2},{4,5},{5,4},{6,7},{7,6},{8,9},{9,8},{10,11... | collective-permute-start | bytes 786440 | tf_op jit(solution)/shard_map/ppermute | solution.py:282
  193.9 17.7 %collective-permute-start.34 = (bf16[1,1024,128]{2,1,0:T(8,128)(2,1)}, bf16[1,1024,128]{2,1,0:T(8,128)(2,1)S(1)}, u32[]{:S(2)}, u32[]{:S(2)}) collective-permute-start(bf16[1,1024,128]{2,1,0:T(8,128)(2,1)} %get-tuple-element.114), channel_id=1, source_target_pairs={{0,1},{1,0},{2,3},{3,2},{4,5},{5,4},{6,7},{7,6},{8,9},{9,8},{10,11... | collective-permute-start | bytes 786440 | tf_op jit(solution)/shard_map/ppermute | solution.py:282
  261.4 17.5 %collective-permute-start.37 = (bf16[1,256,768]{2,1,0:T(8,128)(2,1)}, bf16[1,256,768]{2,1,0:T(8,128)(2,1)S(1)}, u32[]{:S(2)}, u32[]{:S(2)}) collective-permute-start(bf16[1,256,768]{2,1,0:T(8,128)(2,1)} %get-tuple-element.163), channel_id=1, source_target_pairs={{0,6},{1,7},{2,0},{3,1},{4,2},{5,3},{6,4},{7,5},{8,14},{9,15},{10,... | collective-permute-start | bytes 1179656 | tf_op jit(solution)/shard_map/ppermute | solution.py:282
  265.5 18.6 %collective-permute-start.39 = (bf16[1,256,768]{2,1,0:T(8,128)(2,1)}, bf16[1,256,768]{2,1,0:T(8,128)(2,1)S(1)}, u32[]{:S(2)}, u32[]{:S(2)}) collective-permute-start(bf16[1,256,768]{2,1,0:T(8,128)(2,1)} %get-tuple-element.164), channel_id=1, source_target_pairs={{0,2},{1,3},{2,4},{3,5},{4,6},{5,7},{6,0},{7,1},{8,10},{9,11},{10,... | collective-permute-start | bytes 1179656 | tf_op jit(solution)/shard_map/ppermute | solution.py:282
  265.5 36.6 %collective-permute-start.38 = (bf16[1,256,768]{2,1,0:T(8,128)(2,1)}, bf16[1,256,768]{2,1,0:T(8,128)(2,1)S(1)}, u32[]{:S(2)}, u32[]{:S(2)}) collective-permute-start(bf16[1,256,768]{2,1,0:T(8,128)(2,1)} %get-tuple-element.165), channel_id=1, source_target_pairs={{0,4},{1,5},{2,6},{3,7},{4,0},{5,1},{6,2},{7,3},{8,12},{9,13},{10,... | collective-permute-start | bytes 1179656 | tf_op jit(solution)/shard_map/ppermute | solution.py:282
  278.9 25.1 %collective-permute-start.45 = (bf16[112,576]{1,0:T(8,128)(2,1)S(1)}, bf16[112,576]{1,0:T(8,128)(2,1)S(1)}, u32[]{:S(2)}, u32[]{:S(2)}) collective-permute-start(bf16[112,576]{1,0:T(8,128)(2,1)S(1)} %bitcast.386), channel_id=1, source_target_pairs={{0,6},{1,7},{2,0},{3,1},{4,2},{5,3},{6,4},{7,5},{8,14},{9,15},{10,... | collective-permute-start | bytes 387080 | tf_op jit(solution)/shard_map/ppermute | solution.py:282
  284.1 21.1 %collective-permute-start.44 = (bf16[112,576]{1,0:T(8,128)(2,1)S(1)}, bf16[112,576]{1,0:T(8,128)(2,1)S(1)}, u32[]{:S(2)}, u32[]{:S(2)}) collective-permute-start(bf16[112,576]{1,0:T(8,128)(2,1)S(1)} %bitcast.387), channel_id=1, source_target_pairs={{0,4},{1,5},{2,6},{3,7},{4,0},{5,1},{6,2},{7,3},{8,12},{9,13},{10,... | collective-permute-start | bytes 387080 | tf_op jit(solution)/shard_map/ppermute | solution.py:282
  311.9 16.2 %collective-permute-start.46 = (bf16[112,2304]{1,0:T(8,128)(2,1)}, bf16[112,2304]{1,0:T(8,128)(2,1)}, u32[]{:S(2)}, u32[]{:S(2)}) collective-permute-start(bf16[112,2304]{1,0:T(8,128)(2,1)} %reshape.426), channel_id=1, source_target_pairs={{0,1},{1,0},{2,3},{3,2},{4,5},{5,4},{6,7},{7,6},{8,9},{9,8},{10,11... | collective-permute-start | bytes 1548296 | tf_op jit(solution)/shard_map/ppermute | solution.py:282
  317.8 16.5 %collective-permute-start.68 = (bf16[2,384,768]{2,1,0:T(8,128)(2,1)}, bf16[2,384,768]{2,1,0:T(8,128)(2,1)}, u32[]{:S(2)}, u32[]{:S(2)}) collective-permute-start(bf16[2,384,768]{2,1,0:T(8,128)(2,1)} %pad_maximum_fusion.8), channel_id=1, source_target_pairs={{0,8},{1,17},{2,10},{3,19},{4,12},{5,21},{6,14},{7,23},{8,0},{9,25... | collective-permute-start | bytes 3538952 | tf_op jit(solution)/shard_map/ppermute | solution.py:480
  322.3 30.9 %collective-permute-start.58 = (bf16[2,96,3072]{2,1,0:T(8,128)(2,1)}, bf16[2,96,3072]{2,1,0:T(8,128)(2,1)}, u32[]{:S(2)}, u32[]{:S(2)}) collective-permute-start(bf16[2,96,3072]{2,1,0:T(8,128)(2,1)} %pad_maximum_fusion.7), channel_id=1, source_target_pairs={{0,8},{1,17},{2,10},{3,19},{4,12},{5,21},{6,14},{7,23},{8,0},{9,25... | collective-permute-start | bytes 3538952 | tf_op jit(solution)/shard_map/ppermute | solution.py:480
  335.5 22.2 %collective-permute-start.69 = (bf16[1,384,768]{2,1,0:T(8,128)(2,1)S(1)}, bf16[1,384,768]{2,1,0:T(8,128)(2,1)S(1)}, u32[]{:S(2)}, u32[]{:S(2)}) collective-permute-start(bf16[1,384,768]{2,1,0:T(8,128)(2,1)S(1)} %add_convert_fusion.5), channel_id=1, source_target_pairs={{0,16},{1,9},{2,18},{3,11},{4,20},{5,13},{6,22},{7,15},{8,24},{9,1... | collective-permute-start | bytes 1769480 | tf_op jit(solution)/shard_map/ppermute | solution.py:480
  362.9 15.8 %collective-permute-start.71 = (bf16[96,768]{1,0:T(8,128)(2,1)S(1)}, bf16[96,768]{1,0:T(8,128)(2,1)S(1)}, u32[]{:S(2)}, u32[]{:S(2)}) collective-permute-start(bf16[96,768]{1,0:T(8,128)(2,1)S(1)} %get-tuple-element.194), channel_id=1, source_target_pairs={{0,4},{1,5},{2,6},{3,7},{4,0},{5,1},{6,2},{7,3},{8,12},{9,13},{10,... | collective-permute-start | bytes 442376 | tf_op jit(solution)/shard_map/ppermute | solution.py:282
  365.7 20.1 %collective-permute-start.60 = (bf16[24,3072]{1,0:T(8,128)(2,1)S(1)}, bf16[24,3072]{1,0:T(8,128)(2,1)S(1)}, u32[]{:S(2)}, u32[]{:S(2)}) collective-permute-start(bf16[24,3072]{1,0:T(8,128)(2,1)S(1)} %get-tuple-element.201), channel_id=1, source_target_pairs={{0,2},{1,3},{2,4},{3,5},{4,6},{5,7},{6,0},{7,1},{8,10},{9,11},{10,... | collective-permute-start | bytes 442376 | tf_op jit(solution)/shard_map/ppermute | solution.py:282
  365.8 20.7 %collective-permute-start.62 = (bf16[24,3072]{1,0:T(8,128)(2,1)S(1)}, bf16[24,3072]{1,0:T(8,128)(2,1)S(1)}, u32[]{:S(2)}, u32[]{:S(2)}) collective-permute-start(bf16[24,3072]{1,0:T(8,128)(2,1)S(1)} %get-tuple-element.202), channel_id=1, source_target_pairs={{0,6},{1,7},{2,0},{3,1},{4,2},{5,3},{6,4},{7,5},{8,14},{9,15},{10,... | collective-permute-start | bytes 442376 | tf_op jit(solution)/shard_map/ppermute | solution.py:282
  369.6 21.9 %collective-permute-start.61 = (bf16[24,3072]{1,0:T(8,128)(2,1)S(1)}, bf16[24,3072]{1,0:T(8,128)(2,1)S(1)}, u32[]{:S(2)}, u32[]{:S(2)}) collective-permute-start(bf16[24,3072]{1,0:T(8,128)(2,1)S(1)} %get-tuple-element.203), channel_id=1, source_target_pairs={{0,4},{1,5},{2,6},{3,7},{4,0},{5,1},{6,2},{7,3},{8,12},{9,13},{10,... | collective-permute-start | bytes 442376 | tf_op jit(solution)/shard_map/ppermute | solution.py:282
  378.7 17.2 %collective-permute-start.75 = (bf16[96,768]{1,0:T(8,128)(2,1)S(1)}, bf16[96,768]{1,0:T(8,128)(2,1)S(1)}, u32[]{:S(2)}, u32[]{:S(2)}) collective-permute-start(bf16[96,768]{1,0:T(8,128)(2,1)S(1)} %fusion.52), channel_id=1, source_target_pairs={{0,6},{1,7},{2,0},{3,1},{4,2},{5,3},{6,4},{7,5},{8,14},{9,15},{10,... | collective-permute-start | bytes 442376 | tf_op jit(solution)/shard_map/ppermute | solution.py:282
  385.8 19.8 %collective-permute-start.74 = (bf16[96,768]{1,0:T(8,128)(2,1)S(1)}, bf16[96,768]{1,0:T(8,128)(2,1)S(1)}, u32[]{:S(2)}, u32[]{:S(2)}) collective-permute-start(bf16[96,768]{1,0:T(8,128)(2,1)S(1)} %fusion.52), channel_id=1, source_target_pairs={{0,4},{1,5},{2,6},{3,7},{4,0},{5,1},{6,2},{7,3},{8,12},{9,13},{10,... | collective-permute-start | bytes 442376 | tf_op jit(solution)/shard_map/ppermute | solution.py:282
  385.8 19.8 %collective-permute-start.73 = (bf16[96,768]{1,0:T(8,128)(2,1)S(1)}, bf16[96,768]{1,0:T(8,128)(2,1)S(1)}, u32[]{:S(2)}, u32[]{:S(2)}) collective-permute-start(bf16[96,768]{1,0:T(8,128)(2,1)S(1)} %fusion.52), channel_id=1, source_target_pairs={{0,2},{1,3},{2,4},{3,5},{4,6},{5,7},{6,0},{7,1},{8,10},{9,11},{10,... | collective-permute-start | bytes 442376 | tf_op jit(solution)/shard_map/ppermute | solution.py:282
  (84 other events, 860.5 us)
